TPU v7x, 32 devices: a whole 2x2x4 slice. The times are simulated.
32 devices in a mesh: dp: 16 (over z, y, x), seq: 2 (over core).
Axes of the slice: x: 2, y: 2, z: 4, core: 2. Of those that a mesh axis runs over, the one named last changes fastest.
Arguments:
- latents: float32 [2, 16, 256, 16], P(None, 'dp', 'seq'), may hold values from -6 to 6
- noises: float32 [2, 16, 256, 16], P(None, 'dp', 'seq'), may hold values from -6 to 6
- labels: int32 [2, 16], P(None, 'dp'), may hold values from 0 to 999
- dropped: int32 [2, 16], P(None, 'dp'), may hold values 0 or 1
- timesteps: int32 [2, 16], P(None, 'dp'), may hold values from 0 to 999
- layer_in: float32 [1, 1024, 14336], P(None, ('dp', 'seq'))
- layer_out: float32 [1, 4096, 1024], P(None, ('dp', 'seq')), may hold values from -0.09375 to 0.09375
- cond_table: float32 [4361, 1024], P(None, ('dp', 'seq'))
- bias_rows: float32 [19, 1024], P(None, ('dp', 'seq')), may hold values from -1.8 to 1.8
- head_bias: float32 [16], replicated, may hold values from -1.8 to 1.8
- layer_in_m: float32 [1, 1024, 14336], P(None, ('dp', 'seq')), may hold values from -7.1525574e-07 to 7.1525574e-07
- layer_in_v: float32 [1, 1024, 14336], P(None, ('dp', 'seq')), may hold values from 5.351141e-16 to 8.561826e-15
- layer_out_m: float32 [1, 4096, 1024], P(None, ('dp', 'seq')), may hold values from -7.1525574e-07 to 7.1525574e-07
- layer_out_v: float32 [1, 4096, 1024], P(None, ('dp', 'seq')), may hold values from 5.351141e-16 to 8.561826e-15
- cond_table_m: float32 [4361, 1024], P(None, ('dp', 'seq')), may hold values from -7.1525574e-07 to 7.1525574e-07
- cond_table_v: float32 [4361, 1024], P(None, ('dp', 'seq')), may hold values from 5.351141e-16 to 8.561826e-15
- bias_rows_m: float32 [19, 1024], P(None, ('dp', 'seq')), may hold values from -2.861023e-06 to 2.861023e-06
- bias_rows_v: float32 [19, 1024], P(None, ('dp', 'seq')), may hold values from 8.561826e-15 to 1.3698922e-13
- head_bias_m: float32 [16], replicated, may hold values from -2.861023e-06 to 2.861023e-06
- head_bias_v: float32 [16], replicated, may hold values from 8.561826e-15 to 1.3698922e-13
- adam_step: int32 [1], replicated, may hold values from 1 to 20
Outputs:
- loss: float32 [], replicated
- grad_norm: float32 [], replicated
- layer_in_new: float32 [1, 1024, 14336], P(None, ('dp', 'seq'))
- layer_in_m_new: float32 [1, 1024, 14336], P(None, ('dp', 'seq'))
- layer_in_v_new: float32 [1, 1024, 14336], P(None, ('dp', 'seq'))
- layer_out_new: float32 [1, 4096, 1024], P(None, ('dp', 'seq'))
- layer_out_m_new: float32 [1, 4096, 1024], P(None, ('dp', 'seq'))
- layer_out_v_new: float32 [1, 4096, 1024], P(None, ('dp', 'seq'))
- cond_table_new: float32 [4361, 1024], P(None, ('dp', 'seq'))
- cond_table_m_new: float32 [4361, 1024], P(None, ('dp', 'seq'))
- cond_table_v_new: float32 [4361, 1024], P(None, ('dp', 'seq'))
- bias_rows_new: float32 [19, 1024], P(None, ('dp', 'seq'))
- bias_rows_m_new: float32 [19, 1024], P(None, ('dp', 'seq'))
- bias_rows_v_new: float32 [19, 1024], P(None, ('dp', 'seq'))
- head_bias_new: float32 [16], replicated
- head_bias_m_new: float32 [16], replicated
- head_bias_v_new: float32 [16], replicated
All inputs are finite; a program needn't handle non-finite values. No bound on the sum of `dropped` on one device may be relied on, other than what follows from the above.
Results may differ from a plain program's by a relative error of at most 0.0082.
Values may be sent and summed in bfloat16 or wider, within the bound.
A program may use at most 384 MiB of HBM per device.

v0:
```python
from functools import partial
import math

import jax
import jax.numpy as jnp
from jax import lax
from jax.sharding import PartitionSpec as P

D = 1024
HEADS = 16
HEAD_DIM = 64
FF = 4096
CLASSES = 1000
FREQ = 256
PATCH = 16
GRID = 16
LAYERS = 1
MICRO = 2
TOKENS_IMG = 256


clip_limit = 0.005
rate = 0.05
decay = 0.01


def matmul(left, right):
    return jnp.dot(left, right, preferred_element_type=jnp.float32)


def outer_sum(left, right):
    flat_left = left.reshape(-1, left.shape[-1])
    flat_right = right.reshape(-1, right.shape[-1])
    return lax.dot_general(
        flat_left, flat_right, (((0,), (0,)), ((), ())), preferred_element_type=jnp.float32
    )


def back_matmul(grad, weight):
    return lax.dot_general(
        grad, weight, (((grad.ndim - 1,), (1,)), ((), ())), preferred_element_type=jnp.float32
    )


def layer_norm(values):
    centred = values - jnp.mean(values, axis=-1, keepdims=True)
    return centred * lax.rsqrt(jnp.mean(centred * centred, axis=-1, keepdims=True) + 1e-06)


def modulate(values, shift, scale):
    return layer_norm(values) * (1.0 + scale) + shift


def offsets():
    end_class = CLASSES + 1
    end_time_one = end_class + FREQ
    end_time_two = end_time_one + D
    end_patch = end_time_two + PATCH
    end_final = end_patch + 2 * D
    return (end_class, end_time_one, end_time_two, end_patch, end_final)


def positions(row_start, row_count):
    places = row_start + jnp.arange(row_count, dtype=jnp.int32)
    quarter = D // 4
    omegas = 1.0 / 10000.0 ** (jnp.arange(quarter, dtype=jnp.float32) / quarter)
    across = (places // GRID).astype(jnp.float32)[:, None] * omegas[None, :]
    along = (places % GRID).astype(jnp.float32)[:, None] * omegas[None, :]
    return jnp.concatenate(
        [jnp.sin(across), jnp.cos(across), jnp.sin(along), jnp.cos(along)], axis=1
    )


def time_features(time_steps):
    half_freq = FREQ // 2
    rates = jnp.exp(-math.log(10000.0) * jnp.arange(half_freq, dtype=jnp.float32) / half_freq)
    angles = time_steps.astype(jnp.float32)[:, None] * rates[None, :]
    return jnp.concatenate([jnp.cos(angles), jnp.sin(angles)], axis=1)


def signal_levels(time_steps):
    angles = (time_steps.astype(jnp.float32) / 1000.0 + 0.008) / 1.008 * (math.pi / 2.0)
    levels = jnp.cos(angles) ** 2
    return (jnp.sqrt(levels), jnp.sqrt(1.0 - levels))


def split_heads(values):
    return values.reshape(values.shape[0], values.shape[1], HEADS, HEAD_DIM)


def scores_of(queries, keys_values):
    return jnp.einsum(
        "ishd,ikhd->ihsk",
        split_heads(queries),
        split_heads(keys_values[..., :D]),
        preferred_element_type=jnp.float32,
    ) / math.sqrt(HEAD_DIM)


def unstack_layers(piece):
    return jnp.transpose(piece.reshape(piece.shape[0], LAYERS, -1), (1, 0, 2))


def layer_forward(hidden, mods, wide, narrow, rows):
    shift_a, scale_a, gate_a, shift_b, scale_b, gate_b = jnp.split(mods[:, None, :], 6, axis=2)
    normed_a = modulate(hidden, shift_a, scale_a).astype(jnp.bfloat16)
    bias_qkv = jnp.concatenate([rows[0], jnp.zeros((D,), jnp.float32), rows[1]])
    packed = (matmul(normed_a, wide[:, : 3 * D]) + bias_qkv).astype(jnp.bfloat16)
    keys_values = lax.all_gather(packed[..., D:], "seq", axis=1, tiled=True)
    scores = scores_of(packed[..., :D], keys_values)
    row_top = jnp.max(scores, axis=-1, keepdims=True)
    log_total = row_top + jnp.log(jnp.sum(jnp.exp(scores - row_top), axis=-1, keepdims=True))
    probs = jnp.exp(scores - log_total).astype(jnp.bfloat16)
    attended = jnp.einsum(
        "ihsk,ikhd->ishd",
        probs,
        split_heads(keys_values[..., D:]),
        preferred_element_type=jnp.float32,
    )
    attended = attended.reshape(hidden.shape).astype(jnp.bfloat16)
    branch = matmul(attended, wide[:, 3 * D : 4 * D]) + rows[2]
    middle = hidden + gate_a * branch
    normed_b = modulate(middle, shift_b, scale_b).astype(jnp.bfloat16)
    upward = matmul(normed_b, wide[:, 4 * D : 4 * D + FF]) + rows[3:7].reshape(FF)
    downward = matmul(jax.nn.gelu(upward, approximate=True).astype(jnp.bfloat16), narrow) + rows[7]
    saved = (hidden, packed, keys_values, log_total, attended, branch, middle, upward, downward)
    return (middle + gate_b * downward, saved)


def layer_backward(grad_out, saved, mods, wide, narrow):
    hidden, packed, keys_values, log_total, attended, branch, middle, upward, downward = saved
    shift_a, scale_a, gate_a, shift_b, scale_b, gate_b = jnp.split(mods[:, None, :], 6, axis=2)
    grad_gate_b = jnp.sum(grad_out * downward, axis=1)
    grad_down = (gate_b * grad_out).astype(jnp.bfloat16)
    activated, gelu_back = jax.vjp(partial(jax.nn.gelu, approximate=True), upward)
    grad_narrow = outer_sum(activated.astype(jnp.bfloat16), grad_down)
    grad_up = gelu_back(back_matmul(grad_down, narrow))[0].astype(jnp.bfloat16)
    normed_b, norm_back_b = jax.vjp(modulate, middle, shift_b, scale_b)
    grad_fc_one = outer_sum(normed_b.astype(jnp.bfloat16), grad_up)
    grad_mid, grad_shift_b, grad_scale_b = norm_back_b(
        back_matmul(grad_up, wide[:, 4 * D : 4 * D + FF])
    )
    grad_middle = grad_out + grad_mid
    grad_gate_a = jnp.sum(grad_middle * branch, axis=1)
    grad_branch = (gate_a * grad_middle).astype(jnp.bfloat16)
    grad_proj = outer_sum(attended, grad_branch)
    grad_attended = split_heads(
        back_matmul(grad_branch, wide[:, 3 * D : 4 * D]).astype(jnp.bfloat16)
    )
    queries = split_heads(packed[..., :D])
    keys = split_heads(keys_values[..., :D])
    values = split_heads(keys_values[..., D:])
    probs = jnp.exp(scores_of(packed[..., :D], keys_values) - log_total)
    grad_probs = jnp.einsum(
        "ishd,ikhd->ihsk", grad_attended, values, preferred_element_type=jnp.float32
    )
    grad_values = jnp.einsum(
        "ihsk,ishd->ikhd",
        probs.astype(jnp.bfloat16),
        grad_attended,
        preferred_element_type=jnp.float32,
    )
    grad_scores = (
        probs * (grad_probs - jnp.sum(grad_probs * probs, axis=-1, keepdims=True))
    ).astype(jnp.bfloat16)
    head_scale = 1.0 / math.sqrt(HEAD_DIM)
    grad_queries = (
        jnp.einsum("ihsk,ikhd->ishd", grad_scores, keys, preferred_element_type=jnp.float32)
        * head_scale
    )
    grad_keys = (
        jnp.einsum("ihsk,ishd->ikhd", grad_scores, queries, preferred_element_type=jnp.float32)
        * head_scale
    )
    images, rows_all = (keys_values.shape[0], keys_values.shape[1])
    grad_pairs = jnp.concatenate(
        [grad_keys.reshape(images, rows_all, D), grad_values.reshape(images, rows_all, D)], axis=2
    )
    grad_local = lax.psum_scatter(
        grad_pairs.astype(jnp.bfloat16), "seq", scatter_dimension=1, tiled=True
    ).astype(jnp.float32)
    grad_packed = jnp.concatenate([grad_queries.reshape(hidden.shape), grad_local], axis=2).astype(
        jnp.bfloat16
    )
    normed_a, norm_back_a = jax.vjp(modulate, hidden, shift_a, scale_a)
    grad_qkv = outer_sum(normed_a.astype(jnp.bfloat16), grad_packed)
    grad_hid, grad_shift_a, grad_scale_a = norm_back_a(back_matmul(grad_packed, wide[:, : 3 * D]))
    grad_mods = jnp.concatenate(
        [
            grad_shift_a[:, 0],
            grad_scale_a[:, 0],
            grad_gate_a,
            grad_shift_b[:, 0],
            grad_scale_b[:, 0],
            grad_gate_b,
        ],
        axis=1,
    )
    packed_sums = jnp.sum(grad_packed, axis=(0, 1), dtype=jnp.float32)
    bias_grads = jnp.concatenate(
        [
            packed_sums[:D][None],
            packed_sums[2 * D :][None],
            jnp.sum(grad_branch, axis=(0, 1), dtype=jnp.float32)[None],
            jnp.sum(grad_up, axis=(0, 1), dtype=jnp.float32).reshape(FF // D, D),
            jnp.sum(grad_down, axis=(0, 1), dtype=jnp.float32)[None],
        ],
        axis=0,
    )
    return (
        grad_middle + grad_hid,
        grad_mods,
        (grad_qkv, grad_proj, grad_fc_one, grad_narrow, bias_grads),
    )


def forward_pass(
    weights, latent, noise_draw, class_ids, drop_flags, time_steps, head_bias, seq_index
):
    wide_all, narrow_all, table, biases = weights
    end_class, end_time_one, end_time_two, end_patch, end_final = offsets()
    bias_base = 14 * LAYERS
    bias_all = biases.astype(jnp.float32)
    keep_level, spread = signal_levels(time_steps)
    noisy = (keep_level[:, None, None] * latent + spread[:, None, None] * noise_draw).astype(
        jnp.bfloat16
    )
    freqs = time_features(time_steps).astype(jnp.bfloat16)
    time_one = matmul(freqs, table[end_class:end_time_one]) + bias_all[bias_base + 1]
    time_act = jax.nn.silu(time_one).astype(jnp.bfloat16)
    chosen = jnp.where(drop_flags == 1, CLASSES, class_ids)
    choose = (chosen[:, None] == jnp.arange(CLASSES + 1, dtype=jnp.int32)[None, :]).astype(
        jnp.bfloat16
    )
    condition = (
        matmul(time_act, table[end_time_one:end_time_two])
        + bias_all[bias_base + 2]
        + matmul(choose, table[:end_class])
    )
    cond_act = jax.nn.silu(condition).astype(jnp.bfloat16)
    mods_all = [matmul(cond_act, wide_all[0][:, 4 * D + FF :]) + bias_all[8:14].reshape(6 * D)]
    final_shift = matmul(cond_act, table[end_patch : end_patch + D]) + bias_all[bias_base + 3]
    final_scale = matmul(cond_act, table[end_patch + D : end_final]) + bias_all[bias_base + 4]
    rows_local = latent.shape[1]
    hidden = (
        matmul(noisy, table[end_time_two:end_patch])
        + bias_all[bias_base]
        + positions(seq_index * rows_local, rows_local)
    )
    hidden, saved = layer_forward(hidden, mods_all[0], wide_all[0], narrow_all[0], bias_all[0:14])
    layer_saves = [saved]
    normed = modulate(hidden, final_shift[:, None], final_scale[:, None]).astype(jnp.bfloat16)
    predicted = (
        lax.dot_general(
            normed, table[end_final:], (((2,), (1,)), ((), ())), preferred_element_type=jnp.float32
        )
        + head_bias
    )
    return (
        noisy,
        freqs,
        time_one,
        time_act,
        choose,
        condition,
        cond_act,
        mods_all,
        final_shift,
        final_scale,
        hidden,
        normed,
        predicted,
        layer_saves,
    )


def backward_pass(weights, context, noise_draw, norm_count, seq_index):
    wide_all, narrow_all, table, biases = weights
    (
        noisy,
        freqs,
        time_one,
        time_act,
        choose,
        condition,
        cond_act,
        mods_all,
        final_shift,
        final_scale,
        hidden,
        normed,
        predicted,
        layer_saves,
    ) = context
    end_class, end_time_one, end_time_two, end_patch, end_final = offsets()
    differ = predicted - noise_draw
    loss_part = jnp.sum(differ * differ) / norm_count
    grad_pred = (2.0 * differ / norm_count).astype(jnp.bfloat16)
    head_grad = jnp.sum(grad_pred, axis=(0, 1), dtype=jnp.float32)
    grad_out_rows = outer_sum(grad_pred, normed)
    _, final_back = jax.vjp(modulate, hidden, final_shift[:, None], final_scale[:, None])
    grad_hidden, grad_fshift, grad_fscale = final_back(matmul(grad_pred, table[end_final:]))
    mods_grads = [None] * LAYERS
    layer_grads = [None] * LAYERS
    for layer in reversed(range(LAYERS)):
        grad_hidden, mods_grads[layer], layer_grads[layer] = layer_backward(
            grad_hidden, layer_saves[layer], mods_all[layer], wide_all[layer], narrow_all[layer]
        )
    grad_embed = grad_hidden.astype(jnp.bfloat16)
    grad_patch = outer_sum(noisy, grad_embed)
    summed_mods, summed_final = (
        lax.psum(jnp.stack(mods_grads).astype(jnp.bfloat16), "seq").astype(jnp.float32),
        lax.psum(
            jnp.concatenate([grad_fshift[:, 0], grad_fscale[:, 0]], axis=1).astype(jnp.bfloat16),
            "seq",
        ).astype(jnp.float32),
    )
    owner = (seq_index == 0).astype(jnp.float32)
    mods_low = summed_mods.astype(jnp.bfloat16)
    final_low = summed_final.astype(jnp.bfloat16)
    grad_cond_act = back_matmul(final_low[:, :D], table[end_patch : end_patch + D]) + back_matmul(
        final_low[:, D:], table[end_patch + D : end_final]
    )
    layer = 0
    grad_cond_act = grad_cond_act + back_matmul(mods_low[layer], wide_all[layer][:, 4 * D + FF :])
    _, silu_back = jax.vjp(jax.nn.silu, condition)
    grad_condition = silu_back(grad_cond_act)[0].astype(jnp.bfloat16)
    _, silu_back_time = jax.vjp(jax.nn.silu, time_one)
    grad_time = silu_back_time(back_matmul(grad_condition, table[end_time_one:end_time_two]))[
        0
    ].astype(jnp.bfloat16)
    grad_ada = outer_sum(cond_act, mods_low[0]) * owner
    wide_parts = tuple((layer_grads[0][part] for part in range(3))) + (grad_ada,)
    grad_narrow = jnp.concatenate([layer_grads[0][3]], axis=1)
    table_parts = (
        outer_sum(choose, grad_condition) * owner,
        outer_sum(freqs, grad_time) * owner,
        outer_sum(time_act, grad_condition) * owner,
        grad_patch,
        outer_sum(cond_act, final_low[:, :D]) * owner,
        outer_sum(cond_act, final_low[:, D:]) * owner,
        grad_out_rows,
    )
    bias_parts = []
    layer = 0
    bias_parts.append(layer_grads[layer][4])
    bias_parts.append(jnp.sum(mods_low[layer], axis=0, dtype=jnp.float32).reshape(6, D) * owner)
    bias_parts.append(jnp.sum(grad_embed, axis=(0, 1), dtype=jnp.float32)[None])
    bias_parts.append(jnp.sum(grad_time, axis=0, dtype=jnp.float32)[None] * owner)
    bias_parts.append(jnp.sum(grad_condition, axis=0, dtype=jnp.float32)[None] * owner)
    bias_parts.append(jnp.sum(final_low, axis=0, dtype=jnp.float32).reshape(2, D) * owner)
    return (
        wide_parts,
        grad_narrow,
        table_parts,
        jnp.concatenate(bias_parts, axis=0),
        loss_part,
        head_grad,
    )


def adam(weight, grad, first_m, second_m, factor, step_count):
    clipped = grad * factor
    first_new = 0.9 * first_m + 0.1 * clipped
    second_new = 0.999 * second_m + 0.001 * clipped * clipped
    first_hat = first_new / (1.0 - 0.9**step_count)
    second_hat = second_new / (1.0 - 0.999**step_count)
    updated = weight - rate * (first_hat / (jnp.sqrt(second_hat) + 1e-08) + decay * weight)
    return (updated, first_new, second_new)


def shards(
    latents,
    noises,
    labels,
    dropped,
    timesteps,
    layer_in,
    layer_out,
    cond_table,
    bias_rows,
    head_bias,
    layer_in_m,
    layer_in_v,
    layer_out_m,
    layer_out_v,
    cond_table_m,
    cond_table_v,
    bias_rows_m,
    bias_rows_v,
    head_bias_m,
    head_bias_v,
    adam_step,
):
    seq_index = lax.axis_index("seq")
    norm_count = float(MICRO * latents.shape[1] * lax.axis_size("dp") * TOKENS_IMG * PATCH)
    wide_low = layer_in.astype(jnp.bfloat16)
    narrow_low = layer_out.astype(jnp.bfloat16)
    table_low = cond_table.astype(jnp.bfloat16)
    bias_low = bias_rows.astype(jnp.bfloat16)
    totals = None
    loss_sum = jnp.zeros((), jnp.float32)
    head_sum = jnp.zeros((PATCH,), jnp.float32)
    for micro in range(MICRO):
        forward_weights = (
            lax.all_gather(wide_low, ("dp", "seq"), axis=1, tiled=True),
            lax.all_gather(narrow_low, ("dp", "seq"), axis=1, tiled=True),
            lax.all_gather(table_low, ("dp", "seq"), axis=1, tiled=True),
            lax.all_gather(bias_low, ("dp", "seq"), axis=1, tiled=True),
        )
        context = forward_pass(
            forward_weights,
            latents[micro],
            noises[micro],
            labels[micro],
            dropped[micro],
            timesteps[micro],
            head_bias,
            seq_index,
        )
        backward_weights = (
            lax.all_gather(wide_low, ("dp", "seq"), axis=1, tiled=True),
            lax.all_gather(narrow_low, ("dp", "seq"), axis=1, tiled=True),
            lax.all_gather(table_low, ("dp", "seq"), axis=1, tiled=True),
            lax.all_gather(bias_low, ("dp", "seq"), axis=1, tiled=True),
        )
        wide_parts, grad_narrow, table_parts, grad_biases, loss_part, head_grad = backward_pass(
            backward_weights, context, noises[micro], norm_count, seq_index
        )
        pieces = (
            wide_parts[0],
            wide_parts[1],
            wide_parts[2],
            wide_parts[3],
            grad_narrow,
            table_parts[0],
            table_parts[1],
            table_parts[2],
            table_parts[3],
            table_parts[4],
            table_parts[5],
            table_parts[6],
            grad_biases,
        )
        reduced = (
            lax.psum_scatter(pieces[0], ("dp", "seq"), scatter_dimension=0, tiled=True),
            lax.psum_scatter(pieces[1], ("dp", "seq"), scatter_dimension=0, tiled=True),
            lax.psum_scatter(pieces[2], ("dp", "seq"), scatter_dimension=0, tiled=True),
            lax.psum_scatter(pieces[3], ("dp", "seq"), scatter_dimension=0, tiled=True),
            lax.psum_scatter(pieces[4], ("dp", "seq"), scatter_dimension=0, tiled=True),
            lax.psum_scatter(pieces[5], ("dp", "seq"), scatter_dimension=1, tiled=True),
            lax.psum_scatter(pieces[6], ("dp", "seq"), scatter_dimension=1, tiled=True),
            lax.psum_scatter(pieces[7], ("dp", "seq"), scatter_dimension=1, tiled=True),
            lax.psum_scatter(pieces[8], ("dp", "seq"), scatter_dimension=1, tiled=True),
            lax.psum_scatter(pieces[9], ("dp", "seq"), scatter_dimension=1, tiled=True),
            lax.psum_scatter(pieces[10], ("dp", "seq"), scatter_dimension=1, tiled=True),
            lax.psum_scatter(pieces[11], ("dp", "seq"), scatter_dimension=1, tiled=True),
            lax.psum_scatter(pieces[12], ("dp", "seq"), scatter_dimension=1, tiled=True),
        )
        totals = (
            reduced
            if totals is None
            else tuple((first + second for first, second in zip(totals, reduced)))
        )
        loss_sum = loss_sum + loss_part
        head_sum = head_sum + head_grad
    loss_total, head_total = lax.psum((loss_sum, head_sum), ("dp", "seq"))
    grad_wide = jnp.concatenate([unstack_layers(piece) for piece in totals[0:4]], axis=2)
    grad_narrow_all = unstack_layers(totals[4])
    grad_table = jnp.concatenate(totals[5:12], axis=0)
    grad_bias = totals[12]
    local_squares = (
        jnp.sum(grad_wide * grad_wide)
        + jnp.sum(grad_narrow_all * grad_narrow_all)
        + jnp.sum(grad_table * grad_table)
        + jnp.sum(grad_bias * grad_bias)
    )
    squares = lax.psum(local_squares, ("dp", "seq"))
    norm = jnp.sqrt(squares + jnp.sum(head_total * head_total))
    factor = jnp.minimum(1.0, clip_limit / (norm + 1e-06))
    step_count = adam_step[0].astype(jnp.float32)
    results = [loss_total, norm]
    results.extend(adam(layer_in, grad_wide, layer_in_m, layer_in_v, factor, step_count))
    results.extend(adam(layer_out, grad_narrow_all, layer_out_m, layer_out_v, factor, step_count))
    results.extend(adam(cond_table, grad_table, cond_table_m, cond_table_v, factor, step_count))
    results.extend(adam(bias_rows, grad_bias, bias_rows_m, bias_rows_v, factor, step_count))
    results.extend(adam(head_bias, head_total, head_bias_m, head_bias_v, factor, step_count))
    return tuple(results)


def solution(mesh):
    in_specs = (
        P(None, "dp", "seq", None),
        P(None, "dp", "seq", None),
        P(None, "dp"),
        P(None, "dp"),
        P(None, "dp"),
        P(None, ("dp", "seq"), None),
        P(None, ("dp", "seq"), None),
        P(None, ("dp", "seq")),
        P(None, ("dp", "seq")),
        P(),
        P(None, ("dp", "seq"), None),
        P(None, ("dp", "seq"), None),
        P(None, ("dp", "seq"), None),
        P(None, ("dp", "seq"), None),
        P(None, ("dp", "seq")),
        P(None, ("dp", "seq")),
        P(None, ("dp", "seq")),
        P(None, ("dp", "seq")),
        P(),
        P(),
        P(),
    )
    out_specs = (
        P(),
        P(),
        P(None, ("dp", "seq"), None),
        P(None, ("dp", "seq"), None),
        P(None, ("dp", "seq"), None),
        P(None, ("dp", "seq"), None),
        P(None, ("dp", "seq"), None),
        P(None, ("dp", "seq"), None),
        P(None, ("dp", "seq")),
        P(None, ("dp", "seq")),
        P(None, ("dp", "seq")),
        P(None, ("dp", "seq")),
        P(None, ("dp", "seq")),
        P(None, ("dp", "seq")),
        P(),
        P(),
        P(),
    )
    return jax.shard_map(shards, mesh=mesh, in_specs=in_specs, out_specs=out_specs, check_vma=False)
```

profile of v0, /device:TPU:0, one launch (start us, length us, event | category | flops | bytes accessed | tf_op | source)
XLA Modules:
  0.0 2622.7 jit_solution(18160276875415496878)
XLA Ops:
  19.0 44.2 %all-gather = bf16[32,32,19]{1,2,0:T(8,128)(2,1)S(1)} all-gather(bf16[1,32,19]{1,2,0:T(8,128)(2,1)S(1)} %convert_bitcast_fusion), channel_id=1, replica_groups=mesh['dp'=16,'seq'=2] {'dp','seq'}, dimensions={0}, use_global_device_ids=true | all-gather | bytes 40128 | tf_op jit(solution)/shard_map/all_gather | solution.py:409
  64.6 31.0 %all-gather.7.cloned.1.call-done = bf16[4361,1024]{0,1:T(8,128)(2,1)} async-done(((bf16[4361,32]{0,1:T(8,128)(2,1)}), bf16[4361,1024]{0,1:T(8,128)(2,1)}) %all-gather.7.cloned.1.call-update) | async-done | bytes 8931344 | tf_op jit(solution)/shard_map/all_gather | solution.py:408
  113.5 158.9 %all-gather.9.cloned.1.call-done = bf16[1,1024,14336]{2,1,0:T(8,128)(2,1)} async-done(((bf16[1,32,14336]{2,1,0:T(8,128)(2,1)}), bf16[1,1024,14336]{2,1,0:T(8,128)(2,1)}) %all-gather.9.cloned.1.call-update) | async-done | bytes 29360144 | tf_op jit(solution)/shard_map/all_gather | solution.py:406
  272.4 5.5 fusion.12
  277.9 5.5 fusion.14
  315.4 6.1 fusion.24
  321.5 56.2 %all-gather.13.cloned.1.call-done = bf16[1,4096,1024]{2,1,0:T(8,128)(2,1)} async-done(((bf16[1,128,1024]{2,1,0:T(8,128)(2,1)}), bf16[1,4096,1024]{2,1,0:T(8,128)(2,1)}) %all-gather.13.cloned.1.call-update) | async-done | bytes 8388624 | tf_op jit(solution)/shard_map/all_gather | solution.py:407
  377.7 5.8 fusion.302
  392.9 7.4 multiply_reduce_fusion.16
  453.1 7.4 multiply_reduce_fusion.12
  490.7 5.8 multiply_reduce_fusion.7
  514.3 6.6 fusion.8
  520.8 6.4 fusion.10
  567.7 9.7 convolution_add_fusion
  585.2 6.5 convolution_add_fusion.2
  595.5 8.2 convolution_add_fusion.1
  603.9 14.0 add_multiply_fusion
  620.2 58.5 %reduce-scatter.54.cloned.1.call-done = f32[32,19]{1,0:T(8,128)} async-done(((f32[1024,19]{1,0:T(8,128)}), f32[32,19]{1,0:T(8,128)}) %reduce-scatter.54.cloned.1.call-update) | async-done | bytes 2448
  680.1 131.5 %reduce-scatter.52.cloned.1.call-done = f32[32,16]{1,0:T(8,128)} async-done(((f32[1024,16]{1,0:T(8,128)}), f32[32,16]{1,0:T(8,128)}) %reduce-scatter.52.cloned.1.call-update) | async-done | bytes 2064
  811.6 132.3 %reduce-scatter.50.cloned.1.call-done = f32[32,16]{1,0:T(8,128)} async-done(((f32[1024,16]{1,0:T(8,128)}), f32[32,16]{1,0:T(8,128)}) %reduce-scatter.50.cloned.1.call-update) | async-done | bytes 2064
  943.9 133.7 %reduce-scatter.38.cloned.1.call-done = f32[256,32]{0,1:T(8,128)} async-done(((f32[256,1024]{0,1:T(8,128)}), f32[256,32]{0,1:T(8,128)}) %reduce-scatter.38.cloned.1.call-update) | async-done | bytes 32784 | tf_op jit(solution)/shard_map/reduce_scatter | solution.py:452
  1077.6 139.0 %reduce-scatter.36.cloned.1.call-done = f32[1001,32]{0,1:T(8,128)} async-done(((f32[1001,1024]{0,1:T(8,128)}), f32[1001,32]{0,1:T(8,128)}) %reduce-scatter.36.cloned.1.call-update) | async-done | bytes 128144 | tf_op jit(solution)/shard_map/reduce_scatter | solution.py:451
  1216.6 139.3 %reduce-scatter.40.cloned.1.call-done = f32[1024,32]{0,1:T(8,128)} async-done(((f32[1024,1024]{0,1:T(8,128)}), f32[1024,32]{0,1:T(8,128)}) %reduce-scatter.40.cloned.1.call-update) | async-done | bytes 131088 | tf_op jit(solution)/shard_map/reduce_scatter | solution.py:453
  1355.9 139.0 %reduce-scatter.44.cloned.1.call-done = f32[1024,32]{0,1:T(8,128)} async-done(((f32[1024,1024]{0,1:T(8,128)}), f32[1024,32]{0,1:T(8,128)}) %reduce-scatter.44.cloned.1.call-update) | async-done | bytes 131088 | tf_op jit(solution)/shard_map/reduce_scatter | solution.py:456
  1494.9 138.9 %reduce-scatter.42.cloned.1.call-done = f32[1024,32]{0,1:T(8,128)} async-done(((f32[1024,1024]{0,1:T(8,128)}), f32[1024,32]{0,1:T(8,128)}) %reduce-scatter.42.cloned.1.call-update) | async-done | bytes 131088 | tf_op jit(solution)/shard_map/reduce_scatter | solution.py:455
  1636.0 178.8 %reduce-scatter.34.cloned.1.call-done = f32[128,1024]{1,0:T(8,128)} async-done(((f32[4096,1024]{1,0:T(8,128)}), f32[128,1024]{1,0:T(8,128)}) %reduce-scatter.34.cloned.1.call-update) | async-done | bytes 524304 | tf_op jit(solution)/shard_map/reduce_scatter | solution.py:450
  1816.5 143.1 %reduce-scatter.28.cloned.1.call-done = f32[32,1024]{1,0:T(8,128)} async-done(((f32[1024,1024]{1,0:T(8,128)}), f32[32,1024]{1,0:T(8,128)}) %reduce-scatter.28.cloned.1.call-update) | async-done | bytes 131088 | tf_op jit(solution)/shard_map/reduce_scatter | solution.py:447
  1959.6 157.2 %reduce-scatter.26.cloned.1.call-done = f32[32,3072]{1,0:T(8,128)} async-done(((f32[1024,3072]{1,0:T(8,128)}), f32[32,3072]{1,0:T(8,128)}) %reduce-scatter.26.cloned.1.call-update) | async-done | bytes 393232 | tf_op jit(solution)/shard_map/reduce_scatter | solution.py:446
  2116.8 184.2 %reduce-scatter.30.cloned.1.call-done = f32[32,4096]{1,0:T(8,128)} async-done(((f32[1024,4096]{1,0:T(8,128)}), f32[32,4096]{1,0:T(8,128)}) %reduce-scatter.30.cloned.1.call-update) | async-done | bytes 524304 | tf_op jit(solution)/shard_map/reduce_scatter | solution.py:448
  2301.0 254.6 %reduce-scatter.32.cloned.1.call-done = f32[32,6144]{1,0:T(8,128)} async-done(((f32[1024,6144]{1,0:T(8,128)}), f32[32,6144]{1,0:T(8,128)}) %reduce-scatter.32.cloned.1.call-update) | async-done | bytes 786448 | tf_op jit(solution)/shard_map/reduce_scatter | solution.py:449
  2561.0 40.4 %all-reduce = (f32[]{:T(128)}, f32[]{:T(128)}, f32[16]{0:T(128)S(1)}) all-reduce(f32[]{:T(128)S(6)} %add.804, f32[]{:T(128)S(6)} %add.832, f32[16]{0:T(128)S(1)} %add.833), channel_id=1, replica_groups=mesh['dp'=16,'seq'=2] {'dp','seq'}, use_global_device_ids=true, to_apply=%region_18.19 | all-reduce | flops 18 | bytes 144 | tf_op jit(solution)/shard_map/psum | solution.py:467
  2607.5 5.5 multiply_subtract_fusion
  (593 shorter events, 232.9 us)
Async XLA Ops:
  7.2 88.4 %all-gather.7.cloned.1.call-start = ((), (), s32[]{:S(2)}) async-start(), calls=%async_computation.15 | async-start | bytes 9461760 | tf_op jit(solution)/shard_map/all_gather | solution.py:408
  9.1 263.3 %all-gather.9.cloned.1.call-start = ((), (), s32[]{:S(2)}) async-start(), calls=%async_computation.16 | async-start | bytes 30277632 | tf_op jit(solution)/shard_map/all_gather | solution.py:406
  11.7 296.0 %all-gather.11.cloned.1.call-start = ((), (), s32[]{:S(2)}) async-start(), calls=%async_computation.17 | async-start | bytes 1572864 | tf_op jit(solution)/shard_map/all_gather | solution.py:109
  63.5 314.2 %copy-start.115 = (f32[1,1024]{1,0:T(1,128)}, f32[1,1024]{1,0:T(1,128)S(1)}, u32[]{:S(2)}) copy-start(f32[1,1024]{1,0:T(1,128)S(1)} %get-tuple-element.121) | copy-start | bytes 12292
  96.9 215.2 %copy-start.4 = (f32[128,1024]{1,0:T(8,128)}, f32[128,1024]{1,0:T(8,128)S(1)}, u32[]{:S(2)}) copy-start(f32[128,1024]{1,0:T(8,128)S(1)} %get-tuple-element.161) | copy-start | bytes 1572868
  97.0 411.2 %copy-start.94 = (f32[128]{0:T(128)}, f32[128]{0:T(128)S(1)}, u32[]{:S(2)}) copy-start(f32[128]{0:T(128)S(1)} %broadcast_multiply_fusion.7) | copy-start | bytes 1540
  97.2 186.4 %copy-start.103 = (f32[128]{0:T(128)}, f32[128]{0:T(128)S(1)}, u32[]{:S(2)}) copy-start(f32[128]{0:T(128)S(1)} %fusion.268) | copy-start | bytes 1540
  283.5 224.6 %copy-start.63 = (f32[1,1,1024]{2,1,0:T(1,128)}, f32[1,1,1024]{2,1,0:T(1,128)S(1)}, u32[]{:S(2)}) copy-start(f32[1,1,1024]{2,1,0:T(1,128)S(1)} %get-tuple-element.138) | copy-start | bytes 12292
  288.4 89.3 %all-gather.13.cloned.1.call-start = ((), (), s32[]{:S(2)}) async-start(), calls=%async_computation.18 | async-start | bytes 8650752 | tf_op jit(solution)/shard_map/all_gather | solution.py:407
  289.2 123.3 %all-gather.15.cloned.1.call-start = ((), (), s32[]{:S(2)}) async-start(), calls=%async_computation.19 | async-start | bytes 1572864 | tf_op jit(solution)/shard_map/all_gather | solution.py:109
  301.7 206.4 %copy-start.79 = (f32[1,1,1024]{2,1,0:T(1,128)}, f32[1,1,1024]{2,1,0:T(1,128)S(1)}, u32[]{:S(2)}) copy-start(f32[1,1,1024]{2,1,0:T(1,128)S(1)} %get-tuple-element.130) | copy-start | bytes 12292
  307.6 177.8 %reduce-scatter.46.cloned.1.call-start = ((), (), s32[]{:S(2)}) async-start(), calls=%async_computation.30 | async-start | bytes 1572864
  429.6 67.0 %reduce-scatter.48.cloned.1.call-start = ((), (), s32[]{:S(2)}) async-start(), calls=%async_computation.31 | async-start | bytes 1572864
  481.8 196.9 %reduce-scatter.54.cloned.1.call-start = ((), (), s32[]{:S(2)}) async-start(), calls=%async_computation.34 | async-start | bytes 540672
  545.5 266.1 %reduce-scatter.52.cloned.1.call-start = ((), (), s32[]{:S(2)}) async-start(), calls=%async_computation.33 | async-start | bytes 540672
  547.6 396.3 %reduce-scatter.50.cloned.1.call-start = ((), (), s32[]{:S(2)}) async-start(), calls=%async_computation.32 | async-start | bytes 540672
  550.5 527.2 %reduce-scatter.38.cloned.1.call-start = ((), (), s32[]{:S(2)}) async-start(), calls=%async_computation.26 | async-start | bytes 1081344 | tf_op jit(solution)/shard_map/reduce_scatter | solution.py:452
  551.9 664.7 %reduce-scatter.36.cloned.1.call-start = ((), (), s32[]{:S(2)}) async-start(), calls=%async_computation.25 | async-start | bytes 4325376 | tf_op jit(solution)/shard_map/reduce_scatter | solution.py:451
  554.7 801.2 %reduce-scatter.40.cloned.1.call-start = ((), (), s32[]{:S(2)}) async-start(), calls=%async_computation.27 | async-start | bytes 4325376 | tf_op jit(solution)/shard_map/reduce_scatter | solution.py:453
  558.0 936.9 %reduce-scatter.44.cloned.1.call-start = ((), (), s32[]{:S(2)}) async-start(), calls=%async_computation.29 | async-start | bytes 4325376 | tf_op jit(solution)/shard_map/reduce_scatter | solution.py:456
  562.7 1071.1 %reduce-scatter.42.cloned.1.call-start = ((), (), s32[]{:S(2)}) async-start(), calls=%async_computation.28 | async-start | bytes 4325376 | tf_op jit(solution)/shard_map/reduce_scatter | solution.py:455
  563.3 1251.4 %reduce-scatter.34.cloned.1.call-start = ((), (), s32[]{:S(2)}) async-start(), calls=%async_computation.24 | async-start | bytes 17301504 | tf_op jit(solution)/shard_map/reduce_scatter | solution.py:450
  577.5 1382.1 %reduce-scatter.28.cloned.1.call-start = ((), (), s32[]{:S(2)}) async-start(), calls=%async_computation.21 | async-start | bytes 4325376 | tf_op jit(solution)/shard_map/reduce_scatter | solution.py:447
  582.2 1534.6 %reduce-scatter.26.cloned.1.call-start = ((), (), s32[]{:S(2)}) async-start(), calls=%async_computation.20 | async-start | bytes 12976128 | tf_op jit(solution)/shard_map/reduce_scatter | solution.py:446
  591.8 1709.2 %reduce-scatter.30.cloned.1.call-start = ((), (), s32[]{:S(2)}) async-start(), calls=%async_computation.22 | async-start | bytes 17301504 | tf_op jit(solution)/shard_map/reduce_scatter | solution.py:448
  603.7 1952.0 %reduce-scatter.32.cloned.1.call-start = ((), (), s32[]{:S(2)}) async-start(), calls=%async_computation.23 | async-start | bytes 25952256 | tf_op jit(solution)/shard_map/reduce_scatter | solution.py:449
  618.7 1984.7 %copy-start.112 = (f32[16]{0:T(128)S(1)}, f32[16]{0:T(128)}, u32[]{:S(2)}) copy-start(f32[16]{0:T(128)} %param.30) | copy-start | bytes 196
  618.7 1984.7 %copy-start.139 = (f32[16]{0:T(128)S(1)}, f32[16]{0:T(128)}, u32[]{:S(2)}) copy-start(f32[16]{0:T(128)} %param.40) | copy-start | bytes 196
  618.7 1984.7 %copy-start.140 = (f32[16]{0:T(128)S(1)}, f32[16]{0:T(128)}, u32[]{:S(2)}) copy-start(f32[16]{0:T(128)} %param.39) | copy-start | bytes 196
  620.1 1983.8 %copy-start.78 = (f32[19,32]{1,0:T(8,128)S(1)}, f32[19,32]{1,0:T(8,128)}, u32[]{:S(2)}) copy-start(f32[19,32]{1,0:T(8,128)} %param.29) | copy-start | bytes 7300
  620.1 1983.8 %copy-start.92 = (f32[19,32]{1,0:T(8,128)S(1)}, f32[19,32]{1,0:T(8,128)}, u32[]{:S(2)}) copy-start(f32[19,32]{1,0:T(8,128)} %param.38) | copy-start | bytes 7300
  620.2 1983.8 %copy-start.93 = (f32[19,32]{1,0:T(8,128)S(1)}, f32[19,32]{1,0:T(8,128)}, u32[]{:S(2)}) copy-start(f32[19,32]{1,0:T(8,128)} %param.37) | copy-start | bytes 7300
  (142 other events, 1489.2 us)
Sparse Core Ops, SparseCore 0:
  11.5 84.0 all-gather.6
  99.0 173.3 all-gather.8
  288.5 7.1 all-gather.10
  299.0 78.6 all-gather.12
  379.7 7.6 all-gather.14
  429.7 7.1 reduce-scatter.45
  481.9 7.4 reduce-scatter.47
  545.6 133.0 reduce-scatter.53
  681.6 129.9 reduce-scatter.51
  814.3 129.6 reduce-scatter.49
  946.8 130.7 reduce-scatter.37
  1079.8 136.7 reduce-scatter.35
  1218.9 136.9 reduce-scatter.39
  1358.0 136.8 reduce-scatter.43
  1497.0 136.7 reduce-scatter.41
  1636.0 178.7 reduce-scatter.33
  1816.8 142.6 reduce-scatter.27
  1965.4 151.3 reduce-scatter.25
  2119.2 181.7 reduce-scatter.29
  2308.4 247.1 reduce-scatter.31
where the time goes:
time: 2630 us; the launch traced here: 2620 us
  waiting for transfers between devices  2180 us (83%)
  matrix products  203 us (8%)
  blocking collectives  88.3 us (3%)
  other arithmetic  66.4 us (3%)
  local copies, waits for them, and re-layouts  57.4 us (2%)
  between operations  28.5 us (1%)
    unnamed x25, waiting for transfers between devices  323 us
    reduce_scatter x1, waiting for transfers between devices, shards(): lax.psum_scatter(pieces[3], ('dp', 'seq'), scatter_dimension=0, tiled=True)  255 us
    reduce_scatter x1, waiting for transfers between devices, shards(): lax.psum_scatter(pieces[2], ('dp', 'seq'), scatter_dimension=0, tiled=True)  184 us
    reduce_scatter x1, waiting for transfers between devices, shards(): lax.psum_scatter(pieces[4], ('dp', 'seq'), scatter_dimension=0, tiled=True)  179 us
    all_gather x1, waiting for transfers between devices, shards(): lax.all_gather(wide_low, ('dp', 'seq'), axis=1, tiled=True)  159 us
    reduce_scatter x1, waiting for transfers between devices, shards(): lax.psum_scatter(pieces[0], ('dp', 'seq'), scatter_dimension=0, tiled=True)  157 us
    reduce_scatter x1, waiting for transfers between devices, shards(): lax.psum_scatter(pieces[1], ('dp', 'seq'), scatter_dimension=0, tiled=True)  143 us
    reduce_scatter x1, waiting for transfers between devices, shards(): lax.psum_scatter(pieces[7], ('dp', 'seq'), scatter_dimension=1, tiled=True)  139 us
  transfers between devices with their start and end apart: 20, of which 16 were waited for; matrix products, arithmetic and copies ran while one was open for 9% of the time, Pallas kernels for 0%

commit v1 on v0

v1 whole, which is shorter than its diff:
```python
from functools import partial
import math

import jax
import jax.numpy as jnp
from jax import lax
from jax.experimental import pallas as pl
from jax.experimental.pallas import tpu as pltpu
from jax.sharding import PartitionSpec as P

D = 1024
HEADS = 16
HEAD_DIM = 64
FF = 4096
CLASSES = 1000
FREQ = 256
PATCH = 16
GRID = 16
MICRO = 2
TOKENS_IMG = 256
MAIN = 4 * D + FF
MODS = 6 * D

clip_limit = 0.005
rate = 0.05
decay = 0.01

BOTH = ("dp", "seq")
END_CLASS = CLASSES + 1
END_T1 = END_CLASS + FREQ
END_T2 = END_T1 + D
END_PATCH = END_T2 + PATCH
END_FINAL = END_PATCH + 2 * D


def low(values):
    return values.astype(jnp.bfloat16)


def mm(left, right):
    return jnp.dot(left, right, preferred_element_type=jnp.float32)


def mm_tn(left, right):
    return lax.dot_general(
        left, right, (((0,), (0,)), ((), ())), preferred_element_type=jnp.float32
    )


def mm_nt(left, right):
    return lax.dot_general(
        left, right, (((1,), (1,)), ((), ())), preferred_element_type=jnp.float32
    )


def positions():
    places = jnp.arange(TOKENS_IMG, dtype=jnp.int32)
    quarter = D // 4
    omegas = 1.0 / 10000.0 ** (jnp.arange(quarter, dtype=jnp.float32) / quarter)
    across = (places // GRID).astype(jnp.float32)[:, None] * omegas[None, :]
    along = (places % GRID).astype(jnp.float32)[:, None] * omegas[None, :]
    return jnp.concatenate(
        [jnp.sin(across), jnp.cos(across), jnp.sin(along), jnp.cos(along)], axis=1
    )


def time_features(time_steps):
    half_freq = FREQ // 2
    rates = jnp.exp(-math.log(10000.0) * jnp.arange(half_freq, dtype=jnp.float32) / half_freq)
    angles = time_steps.astype(jnp.float32)[:, None] * rates[None, :]
    return jnp.concatenate([jnp.cos(angles), jnp.sin(angles)], axis=1)


def signal_levels(time_steps):
    angles = (time_steps.astype(jnp.float32) / 1000.0 + 0.008) / 1.008 * (math.pi / 2.0)
    levels = jnp.cos(angles) ** 2
    return (jnp.sqrt(levels), jnp.sqrt(1.0 - levels))


def norm_stats(values):
    centred = values - jnp.mean(values, axis=-1, keepdims=True)
    inverse = lax.rsqrt(jnp.mean(centred * centred, axis=-1, keepdims=True) + 1e-06)
    return (centred * inverse, inverse)


def norm_back(grad, unit, inverse, scale):
    grad_unit = grad * (1.0 + scale)
    mean_one = jnp.mean(grad_unit, axis=-1, keepdims=True)
    mean_two = jnp.mean(grad_unit * unit, axis=-1, keepdims=True)
    grad_values = inverse * (grad_unit - mean_one - unit * mean_two)
    return (
        grad_values,
        jnp.sum(grad, axis=0, keepdims=True),
        jnp.sum(grad * unit, axis=0, keepdims=True),
    )


GELU_A = math.sqrt(2.0 / math.pi)
GELU_B = 0.044715


def gelu_both(values):
    squared = values * values
    bent = jnp.tanh(GELU_A * (values + GELU_B * squared * values))
    out = 0.5 * values * (1.0 + bent)
    slope = 0.5 * (1.0 + bent) + 0.5 * values * (1.0 - bent * bent) * (
        GELU_A * (1.0 + 3.0 * GELU_B * squared)
    )
    return (out, slope)


def silu_slope(values):
    sig = jax.nn.sigmoid(values)
    return sig * (1.0 + values * (1.0 - sig))


def heads_of(values):
    return values.reshape(values.shape[0], HEADS, HEAD_DIM)


def adam(weight, grad, first_m, second_m, factor, step_count):
    clipped = grad * factor
    first_new = 0.9 * first_m + 0.1 * clipped
    second_new = 0.999 * second_m + 0.001 * clipped * clipped
    first_hat = first_new / (1.0 - 0.9**step_count)
    second_hat = second_new / (1.0 - 0.999**step_count)
    updated = weight - rate * (first_hat / (jnp.sqrt(second_hat) + 1e-08) + decay * weight)
    return (updated, first_new, second_new)


ID_TYPE = pl.DeviceIdType.MESH
NEAR_LAG, FAR_LAG, BOTH_LAG, HOP, RS_LAG = 0, 1, 2, 1, 1
LINE = 4


def route():
    me, core = lax.axis_index("dp"), lax.axis_index("seq")
    x, y, z = me % 2, (me // 2) % 2, me // 4
    step_x, step_y = 1 - 2 * x, 2 - 4 * y
    near = me + (1 - core) * step_y + core * step_x
    far = me + (1 - core) * step_x + core * step_y
    both = me + step_x + step_y

    def along(chip, hops):
        return chip + 4 * ((z + hops) % LINE - z)

    return me, core, near, far, both, along


def greet(me, core, near, far, along):
    barrier = pltpu.get_barrier_semaphore()
    peers = [(along(me, k), core) for k in range(1, LINE)]
    peers += [(near, core), (far, core), (me, 1 - core)]
    for peer in peers:
        pl.semaphore_signal(barrier, inc=1, device_id=peer, device_id_type=ID_TYPE)
    pl.semaphore_wait(barrier, len(peers))


def gather_kernel(pieces, *refs):
    count = (len(refs) - 3) // 2
    shards, wholes = refs[:count], refs[count : 2 * count]
    send_sem, recv_sem, own_sem = refs[2 * count :]
    me, core, near, far, both, along = route()

    lines = [me] + [along(me, -k) for k in range(1, LINE)]
    from_near = [near] + [along(near, -k) for k in range(1, LINE)]
    from_far = [far] + [along(far, -k) for k in range(1, LINE)]
    from_both = [both] + [along(both, -k) for k in range(1, LINE)]
    sends = []

    def copy_of(piece, slot, chip, core_of, target, own=False):
        which, cut = pieces[piece]
        there = wholes[which].at[(2 * chip + core_of, *cut)]
        return pltpu.make_async_remote_copy(
            src_ref=shards[which].at[cut] if own else there,
            dst_ref=there,
            send_sem=send_sem.at[piece, slot],
            recv_sem=recv_sem.at[piece, slot],
            device_id=target,
            device_id_type=ID_TYPE,
        )

    def send(piece, slot, chip, target, own=False):
        copy = copy_of(piece, slot, chip, core, target, own)
        copy.start()
        sends.append(copy)

    def arrive(piece, slot, chip, core_of):
        copy_of(piece, slot, chip, core_of, (me, 1 - core)).wait_recv()

    to_next, to_near, to_far, to_core = (along(me, 1), core), (near, core), (far, core), (me, 1 - core)

    def start(piece):
        send(piece, 0, me, to_next, own=True)
        send(piece, 3, me, to_near, own=True)
        send(piece, 7, me, to_far, own=True)
        send(piece, 15, me, to_core, own=True)

    def from_line(k):
        def step(piece):
            arrive(piece, k - 1, lines[k], core)
            if k + 1 < LINE:
                send(piece, k, lines[k], to_next)
            send(piece, 3 + k, lines[k], to_near)
            send(piece, 7 + k, lines[k], to_far)
            send(piece, 15 + k, lines[k], to_core)

        return (HOP * (k - 1), step)

    def by_near(k):
        def step(piece):
            arrive(piece, 3 + k, from_near[k], core)
            send(piece, 11 + k, from_near[k], to_far)
            send(piece, 19 + k, from_near[k], to_core)

        return (HOP * max(k, 1) + NEAR_LAG, step)

    def by_far(k):
        def step(piece):
            arrive(piece, 7 + k, from_far[k], core)
            send(piece, 23 + k, from_far[k], to_core)

        return (HOP * max(k, 1) + FAR_LAG, step)

    def by_both(k):
        def step(piece):
            arrive(piece, 11 + k, from_both[k], core)
            send(piece, 27 + k, from_both[k], to_core)

        return (HOP * max(k, 1) + BOTH_LAG, step)

    def by_core(piece):
        for group, chips in enumerate((lines, from_near, from_far, from_both)):
            for k in range(LINE):
                arrive(piece, 15 + 4 * group + k, chips[k], 1 - core)

    steps = [from_line(k) for k in range(1, LINE)]
    steps += [by_near(k) for k in range(LINE)]
    steps += [by_far(k) for k in range(LINE)]
    steps += [by_both(k) for k in range(LINE)]
    steps.append((HOP * LINE + BOTH_LAG, by_core))

    greet(me, core, near, far, along)
    total = len(pieces)
    for piece in range(total):
        start(piece)
    own = [
        pltpu.make_async_copy(shard, whole.at[2 * me + core], own_sem.at[i])
        for i, (shard, whole) in enumerate(zip(shards, wholes))
    ]
    for copy in own:
        copy.start()
    for turn in range(total + steps[-1][0]):
        for late, step in steps:
            if 0 <= turn - late < total:
                step(turn - late)
    for copy in sends:
        copy.wait_send()
    for copy in own:
        copy.wait()


def gather_weights(shards, n_dev, pieces):
    count = len(shards)
    return pl.pallas_call(
        partial(gather_kernel, pieces),
        out_shape=[jax.ShapeDtypeStruct((n_dev, *s.shape), s.dtype) for s in shards],
        in_specs=[pl.BlockSpec(memory_space=pl.ANY)] * count,
        out_specs=[pl.BlockSpec(memory_space=pl.ANY)] * count,
        scratch_shapes=[
            pltpu.SemaphoreType.DMA((len(pieces), 31)),
            pltpu.SemaphoreType.DMA((len(pieces), 31)),
            pltpu.SemaphoreType.DMA((count,)),
        ],
        compiler_params=pltpu.CompilerParams(collective_id=0, has_side_effects=True),
    )(*shards)


def scatter_kernel(pieces, count, *refs):
    parts, outs = refs[:count], refs[count : 2 * count]
    held, from_core, from_far, from_near, from_line = (
        refs[(2 + i) * count : (3 + i) * count] for i in range(5)
    )
    send_sem, recv_sem, load_sem = refs[7 * count :]
    me, core, near, far, both, along = route()
    chips = [along(chip, -k) for chip in (me, near, far, both) for k in range(LINE)]
    others = [along(chip, -k) for chip in (me, far, near, both) for k in range(LINE)]
    sends = []

    def send(piece, slot, source, target_ref, target):
        copy = pltpu.make_async_remote_copy(
            src_ref=source,
            dst_ref=target_ref,
            send_sem=send_sem.at[piece, slot],
            recv_sem=recv_sem.at[piece, slot],
            device_id=target,
            device_id_type=ID_TYPE,
        )
        copy.start()
        sends.append(copy)

    def arrive(piece, slot, target_ref):
        pltpu.make_async_remote_copy(
            src_ref=target_ref,
            dst_ref=target_ref,
            send_sem=send_sem.at[piece, slot],
            recv_sem=recv_sem.at[piece, slot],
            device_id=(me, 1 - core),
            device_id_type=ID_TYPE,
        ).wait_recv()

    def view(refs_of, piece, j):
        which, cut = pieces[piece]
        return refs_of[which].at[(j, *cut)]

    def load(piece, j):
        which, cut = pieces[piece]
        return pltpu.make_async_copy(
            parts[which].at[(2 * chips[j] + core, *cut)],
            view(held, piece, j),
            load_sem.at[piece, j],
        )

    def add(piece, j, other):
        mine = view(held, piece, j)
        total = mine[...].astype(jnp.float32) + other[...].astype(jnp.float32)
        mine[...] = total.astype(jnp.bfloat16)

    order = [12 + k for k in (1, 2, 3, 0)] + [8 + k for k in (1, 2, 3, 0)]
    order += [4 + k for k in (1, 2, 3, 0)] + [k for k in (1, 2, 3, 0)]

    def begin(piece):
        which, cut = pieces[piece]
        for j in order:
            send(
                piece,
                j,
                parts[which].at[(2 * others[j] + 1 - core, *cut)],
                view(from_core, piece, j),
                (me, 1 - core),
            )
            load(piece, j).start()

    def by_core(piece):
        for j in order:
            load(piece, j).wait()
            arrive(piece, j, view(from_core, piece, j))
            add(piece, j, view(from_core, piece, j))
            if j >= 8:
                send(piece, 16 + j - 8, view(held, piece, j), view(from_far, piece, j - 8), (far, core))

    def by_far(piece):
        for j in order[8:]:
            arrive(piece, 16 + j, view(from_far, piece, j))
            add(piece, j, view(from_far, piece, j))
            if j >= 4:
                send(piece, 24 + j - 4, view(held, piece, j), view(from_near, piece, j - 4), (near, core))

    def by_near(piece):
        for j in order[12:]:
            arrive(piece, 24 + j, view(from_near, piece, j))
            add(piece, j, view(from_near, piece, j))
            if j:
                send(piece, 27 + j, view(held, piece, j), view(from_line, piece, j - 1), (along(me, -j), core))

    def by_line(piece):
        which, cut = pieces[piece]
        total = view(held, piece, 0)[...].astype(jnp.float32)
        for j in range(1, LINE):
            arrive(piece, 27 + j, view(from_line, piece, j - 1))
            total = total + view(from_line, piece, j - 1)[...].astype(jnp.float32)
        outs[which][cut] = total

    greet(me, core, near, far, along)
    total = len(pieces)
    for piece in range(total):
        begin(piece)
    steps = [(0, by_core), (RS_LAG, by_far), (2 * RS_LAG, by_near), (3 * RS_LAG, by_line)]
    for turn in range(total + steps[-1][0]):
        for late, step in steps:
            if 0 <= turn - late < total:
                step(turn - late)
    for copy in sends:
        copy.wait_send()


def scatter_grads(parts, pieces, call_id):
    count = len(parts)
    shards = [p.shape[1:] for p in parts]
    return pl.pallas_call(
        partial(scatter_kernel, pieces, count),
        out_shape=[jax.ShapeDtypeStruct(s, jnp.float32) for s in shards],
        in_specs=[pl.BlockSpec(memory_space=pl.ANY)] * count,
        out_specs=[pl.BlockSpec(memory_space=pltpu.VMEM)] * count,
        scratch_shapes=[
            *(pltpu.VMEM((blocks, *s), jnp.bfloat16) for blocks in (16, 16, 8, 4, 3) for s in shards),
            pltpu.SemaphoreType.DMA((len(pieces), 31)),
            pltpu.SemaphoreType.DMA((len(pieces), 31)),
            pltpu.SemaphoreType.DMA((len(pieces), 16)),
        ],
        compiler_params=pltpu.CompilerParams(
            collective_id=call_id, has_side_effects=True, vmem_limit_bytes=56 * 2**20
        ),
    )(*parts)


def exchange_kernel(kinds, n_dev, *refs):
    count = len(kinds)
    sources, outs = refs[:count], refs[count : 2 * count]
    send_sem, recv_sem = refs[2 * count :]
    me = 2 * lax.axis_index("dp") + lax.axis_index("seq")
    others = [(me + k) % n_dev for k in range(1, n_dev)]
    barrier = pltpu.get_barrier_semaphore()
    for other in others:
        pl.semaphore_signal(barrier, inc=1, device_id=(other // 2, other % 2), device_id_type=ID_TYPE)
    pl.semaphore_wait(barrier, n_dev - 1)

    def copy_of(i, k, other, block):
        return pltpu.make_async_remote_copy(
            src_ref=sources[i] if kinds[i] == "all" else sources[i].at[other],
            dst_ref=outs[i].at[block],
            send_sem=send_sem.at[i, k],
            recv_sem=recv_sem.at[i, k],
            device_id=(other // 2, other % 2),
            device_id_type=ID_TYPE,
        )

    copies = [copy_of(i, k, other, me) for k, other in enumerate(others) for i in range(count)]
    for copy in copies:
        copy.start()
    for i in range(count):
        outs[i][me] = sources[i][...] if kinds[i] == "all" else sources[i][me]
    for k in range(n_dev - 1):
        sender = (me + n_dev - 1 - k) % n_dev
        for i in range(count):
            copy_of(i, k, sender, sender).wait_recv()
    for copy in copies:
        copy.wait_send()


def exchange(arrays, kinds, n_dev, call_id):
    count = len(arrays)
    return pl.pallas_call(
        partial(exchange_kernel, kinds, n_dev),
        out_shape=[
            jax.ShapeDtypeStruct((n_dev, *a.shape) if kind == "all" else a.shape, a.dtype)
            for a, kind in zip(arrays, kinds)
        ],
        in_specs=[pl.BlockSpec(memory_space=pltpu.VMEM)] * count,
        out_specs=[pl.BlockSpec(memory_space=pltpu.VMEM)] * count,
        scratch_shapes=[
            pltpu.SemaphoreType.DMA((count, n_dev - 1)),
            pltpu.SemaphoreType.DMA((count, n_dev - 1)),
        ],
        compiler_params=pltpu.CompilerParams(
            collective_id=call_id, has_side_effects=True, vmem_limit_bytes=32 * 2**20
        ),
    )(*arrays)

def tiled(parts):
    return parts[0].shape[0] % 16 == 0 and lax.axis_size("dp") == 4 * LINE


def column_cuts(which, columns, step):
    return [(which, (slice(None), slice(c, c + step))) for c in range(0, columns, step)]


def row_cuts(which, rows, step):
    return [(which, (slice(r, r + step), slice(None))) for r in range(0, rows, step)]


def all_weights(main, narrow, n_dev):
    if not tiled([main, narrow]):
        return (
            lax.all_gather(main, BOTH, axis=0, tiled=True),
            lax.all_gather(narrow, BOTH, axis=0, tiled=True),
        )
    pieces = column_cuts(0, MAIN, 1024) + row_cuts(1, FF // n_dev, 32)
    main_all, narrow_all = gather_weights([main, narrow], n_dev, tuple(pieces))
    return main_all.reshape(D, MAIN), narrow_all.reshape(FF, D)


def summed_grads(parts, n_dev):
    blocks = [p.reshape(n_dev, p.shape[0] // n_dev, p.shape[1]) for p in parts]
    if not tiled([b[0] for b in blocks]):
        return [
            lax.psum_scatter(p, BOTH, scatter_dimension=0, tiled=True).astype(jnp.float32)
            for p in parts
        ]
    pieces = row_cuts(0, FF // n_dev, 32)
    for which in range(1, len(parts)):
        pieces += column_cuts(which, parts[which].shape[1], 1024)
    return scatter_grads(blocks, tuple(pieces), 1)


def swap(arrays, kinds, n_dev, call_id):
    if n_dev > 8 * LINE:
        return [
            lax.all_gather(a, BOTH) if kind == "all" else lax.all_to_all(a, BOTH, 0, 0, tiled=True)
            for a, kind in zip(arrays, kinds)
        ]
    return exchange(arrays, kinds, n_dev, call_id)


def shards(
    latents,
    noises,
    labels,
    dropped,
    timesteps,
    layer_in,
    layer_out,
    cond_table,
    bias_rows,
    head_bias,
    layer_in_m,
    layer_in_v,
    layer_out_m,
    layer_out_v,
    cond_table_m,
    cond_table_v,
    bias_rows_m,
    bias_rows_v,
    head_bias_m,
    head_bias_v,
    adam_step,
):
    core = lax.axis_index("seq")
    chips = lax.axis_size("dp")
    n_dev = chips * lax.axis_size("seq")
    me = lax.axis_index("dp") * 2 + core
    norm_count = float(MICRO * chips * TOKENS_IMG * PATCH)
    part = layer_in.shape[1]

    pair = jnp.concatenate([latents[:, 0], noises[:, 0]], axis=2)
    other = lax.dynamic_index_in_dim(pair, 1 - core, 0, keepdims=False)
    mine = lax.dynamic_index_in_dim(pair, core, 0, keepdims=False)
    came = lax.ppermute(other, "seq", [(0, 1), (1, 0)])
    image = jnp.where(core == 0, jnp.concatenate([mine, came]), jnp.concatenate([came, mine]))
    latent, noise = image[:, :PATCH], image[:, PATCH:]

    scalars = jnp.stack([labels[:, 0], dropped[:, 0], timesteps[:, 0]], axis=1)
    scalars = lax.dynamic_slice_in_dim(scalars, core, 1, 0).astype(jnp.float32)
    scalars = jnp.pad(scalars, ((0, 0), (0, 125)))

    main_low = low(layer_in[0, :, :MAIN])
    ada_low = low(layer_in[0, :, MAIN:])
    narrow_low = low(layer_out[0])
    table_low = low(cond_table)
    bias_low = low(bias_rows)
    bias_own = bias_low.astype(jnp.float32)

    small = jnp.concatenate([bias_low, table_low[END_T2:END_PATCH], table_low[END_FINAL:]], axis=0)
    small_all, scalars = swap([small, scalars], ("all", "all"), n_dev, 2)
    small_all = jnp.transpose(small_all, (1, 0, 2)).reshape(-1, D)
    scalars = scalars[:, 0, :3].astype(jnp.int32)
    chosen = jnp.where(scalars[:, 1] == 1, CLASSES, scalars[:, 0])
    times = scalars[:, 2]
    my_time = lax.dynamic_slice_in_dim(times, me, 1)
    bias_all = small_all[:19].astype(jnp.float32)
    patch_w = small_all[19:35]
    out_w = small_all[35:51]
    main_all, narrow_all = all_weights(main_low, narrow_low, n_dev)

    freqs = low(time_features(times))
    time_one = mm(freqs, table_low[END_CLASS:END_T1]) + bias_own[15]
    time_act = low(jax.nn.silu(time_one))
    (time_act_all,) = swap([time_act], ("all",), n_dev, 3)
    time_act_all = jnp.transpose(time_act_all, (1, 0, 2)).reshape(n_dev, D)
    choose = low((chosen[:, None] == jnp.arange(CLASSES + 1, dtype=jnp.int32)[None, :]))
    condition = (
        mm(time_act_all, table_low[END_T1:END_T2])
        + bias_own[16]
        + mm(choose, table_low[:END_CLASS])
    )
    cond_act = low(jax.nn.silu(condition))
    mods_part = low(mm(cond_act, ada_low)).reshape(n_dev, MODS // 128, 128)
    cond_act_all, mods_came = swap([cond_act, mods_part], ("all", "each"), n_dev, 4)
    cond_act_all = jnp.transpose(cond_act_all, (1, 0, 2)).reshape(n_dev, D)
    mods = (
        jnp.sum(mods_came.astype(jnp.float32), axis=0).reshape(1, MODS)
        + bias_all[8:14].reshape(1, MODS)
    )
    final_cols = jnp.concatenate(
        [
            mm(cond_act_all, table_low[END_PATCH : END_PATCH + D]) + bias_own[17],
            mm(cond_act_all, table_low[END_PATCH + D : END_FINAL]) + bias_own[18],
        ],
        axis=1,
    )
    (final_came,) = swap([final_cols[:, None]], ("each",), n_dev, 5)
    final_came = final_came[:, 0]
    f_shift = final_came[:, :part].reshape(1, D)
    f_scale = final_came[:, part:].reshape(1, D)
    shift_a, scale_a, gate_a, shift_b, scale_b, gate_b = jnp.split(mods, 6, axis=1)

    keep_level, spread = signal_levels(my_time)
    noisy = low(keep_level[:, None] * latent + spread[:, None] * noise)
    hidden = mm(noisy, patch_w) + bias_all[14] + positions()
    unit_a, inv_a = norm_stats(hidden)
    normed_a = low(unit_a * (1.0 + scale_a) + shift_a)
    bias_qkv = jnp.concatenate([bias_all[0], jnp.zeros((D,), jnp.float32), bias_all[1]])
    packed = low(mm(normed_a, main_all[:, : 3 * D]) + bias_qkv)
    queries, keys, values = (heads_of(packed[:, i * D : (i + 1) * D]) for i in range(3))
    head_scale = 1.0 / math.sqrt(HEAD_DIM)
    scores = (
        jnp.einsum("shd,khd->hsk", queries, keys, preferred_element_type=jnp.float32) * head_scale
    )
    expd = jnp.exp(scores - jnp.max(scores, axis=-1, keepdims=True))
    probs = expd / jnp.sum(expd, axis=-1, keepdims=True)
    probs_low = low(probs)
    attended = jnp.einsum("hsk,khd->shd", probs_low, values, preferred_element_type=jnp.float32)
    attended = low(attended.reshape(TOKENS_IMG, D))
    branch = mm(attended, main_all[:, 3 * D : 4 * D]) + bias_all[2]
    middle = hidden + gate_a * branch
    unit_b, inv_b = norm_stats(middle)
    normed_b = low(unit_b * (1.0 + scale_b) + shift_b)
    upward = mm(normed_b, main_all[:, 4 * D :]) + bias_all[3:7].reshape(FF)
    activated, slope = gelu_both(upward)
    activated = low(activated)
    downward = mm(activated, narrow_all) + bias_all[7]
    last = middle + gate_b * downward
    unit_f, inv_f = norm_stats(last)
    normed_f = low(unit_f * (1.0 + f_scale) + f_shift)
    predicted = mm_nt(normed_f, out_w) + head_bias

    differ = predicted - noise
    loss_part = jnp.sum(differ * differ) / norm_count
    grad_pred = low(2.0 * differ / norm_count)
    head_part = jnp.sum(grad_pred, axis=0, dtype=jnp.float32)
    grad_out_w = mm_tn(grad_pred, normed_f)
    grad_last, g_fshift, g_fscale = norm_back(mm(grad_pred, out_w), unit_f, inv_f, f_scale)
    g_gate_b = jnp.sum(grad_last * downward, axis=0, keepdims=True)
    grad_down = low(gate_b * grad_last)
    grad_narrow = low(mm_tn(activated, grad_down))
    grad_up = low(slope * mm_nt(grad_down, narrow_all))
    grad_fc1 = low(mm_tn(normed_b, grad_up))
    grad_mid, g_shift_b, g_scale_b = norm_back(
        mm_nt(grad_up, main_all[:, 4 * D :]), unit_b, inv_b, scale_b
    )
    grad_middle = grad_last + grad_mid
    g_gate_a = jnp.sum(grad_middle * branch, axis=0, keepdims=True)
    grad_branch = low(gate_a * grad_middle)
    grad_proj = low(mm_tn(attended, grad_branch))
    grad_att = heads_of(low(mm_nt(grad_branch, main_all[:, 3 * D : 4 * D])))
    grad_probs = jnp.einsum("shd,khd->hsk", grad_att, values, preferred_element_type=jnp.float32)
    grad_values = jnp.einsum("hsk,shd->khd", probs_low, grad_att, preferred_element_type=jnp.float32)
    grad_scores = low(
        probs * (grad_probs - jnp.sum(grad_probs * probs, axis=-1, keepdims=True))
    )
    grad_queries = (
        jnp.einsum("hsk,khd->shd", grad_scores, keys, preferred_element_type=jnp.float32)
        * head_scale
    )
    grad_keys = (
        jnp.einsum("hsk,shd->khd", grad_scores, queries, preferred_element_type=jnp.float32)
        * head_scale
    )
    grad_packed = low(
        jnp.concatenate(
            [g.reshape(TOKENS_IMG, D) for g in (grad_queries, grad_keys, grad_values)], axis=1
        )
    )
    grad_qkv = low(mm_tn(normed_a, grad_packed))
    grad_hid, g_shift_a, g_scale_a = norm_back(
        mm_nt(grad_packed, main_all[:, : 3 * D]), unit_a, inv_a, scale_a
    )
    grad_embed = low(grad_middle + grad_hid)
    grad_patch = mm_tn(noisy, grad_embed)

    grad_narrow, grad_fc1, grad_proj, grad_qkv = summed_grads(
        [grad_narrow, grad_fc1, grad_proj, grad_qkv], n_dev
    )

    mods_grads = low(
        jnp.concatenate(
            [g_shift_a, g_scale_a, g_gate_a, g_shift_b, g_scale_b, g_gate_b, g_fshift, g_fscale],
            axis=1,
        )
    )
    (mods_grads,) = swap([mods_grads.reshape(8 * D // 128, 128)], ("all",), n_dev, 6)
    mods_grads = mods_grads.reshape(n_dev, 8 * D)
    mods_low = mods_grads[:, :MODS]
    cut = mods_grads.reshape(n_dev, 8, n_dev, part)
    own_cols = lax.dynamic_index_in_dim(cut, me, 2, keepdims=False)
    fshift_low, fscale_low = own_cols[:, 6], own_cols[:, 7]
    grad_ada = mm_tn(cond_act, mods_low)
    cond_part = mm_nt(fshift_low, table_low[END_PATCH : END_PATCH + D]) + mm_nt(
        fscale_low, table_low[END_PATCH + D : END_FINAL]
    )
    (cond_came,) = swap([cond_part.reshape(n_dev, n_dev, part).transpose(1, 0, 2)], ("each",), n_dev, 7)
    grad_cond_act = jnp.sum(cond_came, axis=0) + mm_nt(mods_low, ada_low)
    grad_condition = low(grad_cond_act * silu_slope(condition))
    time_part = mm_nt(grad_condition, table_low[END_T1:END_T2])

    row_sums = lambda values: jnp.sum(values.astype(jnp.float32), axis=0, keepdims=True)
    packed_sums = row_sums(grad_packed)
    small_part = jnp.concatenate(
        [
            packed_sums[:, :D],
            packed_sums[:, 2 * D :],
            row_sums(grad_branch),
            row_sums(grad_up).reshape(4, D),
            row_sums(grad_down),
            row_sums(grad_embed),
            grad_patch,
            grad_out_w,
        ],
        axis=0,
    )
    rows_in = small_part.shape[0]
    sums_mine = jnp.pad(jnp.concatenate([loss_part[None], head_part]), (0, 111))[None]
    time_came, small_came, sums_all = swap(
        [
            time_part.reshape(n_dev, n_dev, part).transpose(1, 0, 2),
            small_part.reshape(rows_in, n_dev, part).transpose(1, 0, 2),
            sums_mine,
        ],
        ("each", "each", "all"),
        n_dev,
        8,
    )
    grad_time = low(jnp.sum(time_came, axis=0) * silu_slope(time_one))
    small_came = jnp.sum(small_came, axis=0)
    sums_all = jnp.sum(sums_all[:, 0, :17], axis=0)
    loss_total, head_total = sums_all[0], sums_all[1:]

    grad_table = jnp.concatenate(
        [
            mm_tn(choose, grad_condition),
            mm_tn(freqs, grad_time),
            mm_tn(time_act_all, grad_condition),
            small_came[9:25],
            mm_tn(cond_act_all, fshift_low),
            mm_tn(cond_act_all, fscale_low),
            small_came[25:41],
        ],
        axis=0,
    )
    grad_bias = jnp.concatenate(
        [
            small_came[:8],
            jnp.sum(own_cols[:, :6].astype(jnp.float32), axis=0),
            small_came[8:9],
            row_sums(grad_time),
            row_sums(grad_condition),
            row_sums(fshift_low),
            row_sums(fscale_low),
        ],
        axis=0,
    )
    grad_wide = jnp.concatenate([grad_qkv, grad_proj, grad_fc1, grad_ada], axis=1)[None]
    grad_narrow = grad_narrow[None]

    local_squares = (
        jnp.sum(grad_wide * grad_wide)
        + jnp.sum(grad_narrow * grad_narrow)
        + jnp.sum(grad_table * grad_table)
        + jnp.sum(grad_bias * grad_bias)
    )
    (squares,) = swap([jnp.full((1, 128), local_squares)], ("all",), n_dev, 9)
    squares = jnp.sum(squares[:, 0, 0])
    norm = jnp.sqrt(squares + jnp.sum(head_total * head_total))
    factor = jnp.minimum(1.0, clip_limit / (norm + 1e-06))
    step_count = adam_step[0].astype(jnp.float32)
    results = [loss_total, norm]
    results.extend(adam(layer_in, grad_wide, layer_in_m, layer_in_v, factor, step_count))
    results.extend(adam(layer_out, grad_narrow, layer_out_m, layer_out_v, factor, step_count))
    results.extend(adam(cond_table, grad_table, cond_table_m, cond_table_v, factor, step_count))
    results.extend(adam(bias_rows, grad_bias, bias_rows_m, bias_rows_v, factor, step_count))
    results.extend(adam(head_bias, head_total, head_bias_m, head_bias_v, factor, step_count))
    return tuple(results)


def solution(mesh):
    in_specs = (
        P(None, "dp", "seq", None),
        P(None, "dp", "seq", None),
        P(None, "dp"),
        P(None, "dp"),
        P(None, "dp"),
        P(None, ("dp", "seq"), None),
        P(None, ("dp", "seq"), None),
        P(None, ("dp", "seq")),
        P(None, ("dp", "seq")),
        P(),
        P(None, ("dp", "seq"), None),
        P(None, ("dp", "seq"), None),
        P(None, ("dp", "seq"), None),
        P(None, ("dp", "seq"), None),
        P(None, ("dp", "seq")),
        P(None, ("dp", "seq")),
        P(None, ("dp", "seq")),
        P(None, ("dp", "seq")),
        P(),
        P(),
        P(),
    )
    out_specs = (
        P(),
        P(),
        P(None, ("dp", "seq"), None),
        P(None, ("dp", "seq"), None),
        P(None, ("dp", "seq"), None),
        P(None, ("dp", "seq"), None),
        P(None, ("dp", "seq"), None),
        P(None, ("dp", "seq"), None),
        P(None, ("dp", "seq")),
        P(None, ("dp", "seq")),
        P(None, ("dp", "seq")),
        P(None, ("dp", "seq")),
        P(None, ("dp", "seq")),
        P(None, ("dp", "seq")),
        P(),
        P(),
        P(),
    )
    return jax.shard_map(shards, mesh=mesh, in_specs=in_specs, out_specs=out_specs, check_vma=False)
```

time: 2630 us -> 554 us (0.21)
  waiting for transfers between devices: 2180 us -> 0.01 us
  Pallas kernels: 0 us -> 379 us
  matrix products: 203 us -> 91.4 us
  blocking collectives: 88.3 us -> 0 us
  other arithmetic: 66.4 us -> 35.4 us
    reduce_scatter x10 -> x0, waiting for transfers between devices: 1610 us -> none  [the longest x1 255 us: shards(): lax.psum_scatter(pieces[3], ('dp', 'seq'), scatter_dimension=0, tiled=True)]
    pallas_call x0 -> x10, Pallas kernels: none -> 379 us  [the longest x1 136 us: scatter_grads(): pl.pallas_call(partial(scatter_kernel, pieces, count), out_shape=[jax.Sha...]
    unnamed x25 -> x0, waiting for transfers between devices: 323 us -> none
    all_gather x5 -> x0, waiting for transfers between devices: 246 us -> none  [the longest x1 159 us: shards(): lax.all_gather(wide_low, ('dp', 'seq'), axis=1, tiled=True)]
    dot_general x66 -> x38, matrix products: 203 us -> 87.9 us  [the longest x9 36 us: mm_nt(): lax.dot_general(left, right, (((1,), (1,)), ((), ())), preferred_element_...]
    all_gather x1 -> x0, blocking collectives: 44.2 us -> none  [shards(): lax.all_gather(bias_low, ('dp', 'seq'), axis=1, tiled=True)]
    psum x2 -> x0, blocking collectives: 44.1 us -> none  [the longest x1 40.4 us: shards(): loss_total, head_total = lax.psum((loss_sum, head_sum), ('dp', 'seq'))]
    unnamed x332 -> x192, local copies, waits for them, and re-layouts: 38.5 us -> 10.1 us
  transfers between devices with their start and end apart: 20 -> 1, of which waited for: 16 -> 0; matrix products, arithmetic and copies ran while one was open for 9% -> 4% of each run, Pallas kernels for 0% -> 32%
where the time goes in v1:
time: 554 us; the launch traced here: 548 us
  Pallas kernels  379 us (68%)
  matrix products  91.4 us (16%)
  other arithmetic  35.4 us (6%)
  local copies, waits for them, and re-layouts  32.1 us (6%)
  between operations  9.67 us (2%)
    pallas_call x1, Pallas kernels, scatter_grads(): pl.pallas_call(partial(scatter_kernel, pieces, count), out_shape=[jax.Sha...  136 us
    pallas_call x8, Pallas kernels, exchange(): pl.pallas_call(partial(exchange_kernel, kinds, n_dev), out_shape=[jax.Sha...  128 us
    pallas_call x1, Pallas kernels, gather_weights(): pl.pallas_call(partial(gather_kernel, pieces), out_shape=[jax.ShapeDtypeS...  115 us
    dot_general x9, matrix products, mm_nt(): lax.dot_general(left, right, (((1,), (1,)), ((), ())), preferred_element_...  36 us
    dot_general x12, matrix products, mm_tn(): lax.dot_general(left, right, (((0,), (0,)), ((), ())), preferred_element_...  23.4 us
    dot_general x12, matrix products, mm(): return jnp.dot(left, right, preferred_element_type=jnp.float32)  20.5 us
  transfers between devices with their start and end apart: 1, of which 0 were waited for; matrix products, arithmetic and copies ran while one was open for 4% of the time, Pallas kernels for 32%

profile of v1, /device:TPU:0, one launch (start us, length us, event | category | flops | bytes accessed | tf_op | source)
XLA Modules:
  0.0 548.3 jit_solution(5753567885610074750)
XLA Ops:
  7.3 16.1 %shard_map.332 = (bf16[32,51,32]{2,1,0:T(8,128)(2,1)S(1)}, f32[32,1,128]{2,1,0:T(1,128)S(1)}) custom-call(bf16[51,32]{1,0:T(8,128)(2,1)S(1)} %pad_maximum_fusion.4.refs_0_, f32[1,128]{1,0:T(1,128)S(1)} %pad.8.refs_1_), custom_call_target="tpu_custom_call" | custom-call | tf_op jit(solution)/shard_map/pallas_call | solution.py:443
  29.0 13.1 %shard_map.333 = bf16[32,32,32]{2,1,0:T(8,128)(2,1)S(1)} custom-call(bf16[32,32]{1,0:T(8,128)(2,1)S(1)} %get-tuple-element.167.refs_0_), custom_call_target="tpu_custom_call" | custom-call | tf_op jit(solution)/shard_map/pallas_call | solution.py:443
  45.0 18.9 %shard_map.334 = (bf16[32,32,32]{2,1,0:T(8,128)(2,1)S(1)}, bf16[32,48,128]{2,1,0:T(8,128)(2,1)S(1)}) custom-call(bf16[32,32]{1,0:T(8,128)(2,1)S(1)} %get-tuple-element.169.refs_0_, bf16[32,48,128]{2,1,0:T(8,128)(2,1)S(1)} %bitcast.166), custom_call_target="tpu_custom_call" | custom-call | tf_op jit(solution)/shard_map/pallas_call | solution.py:443
  66.5 11.8 %shard_map.336 = f32[32,1,64]{2,1,0:T(1,128)S(1)} custom-call(f32[32,1,64]{2,1,0:T(1,128)S(1)} %bitcast.173), custom_call_target="tpu_custom_call" | custom-call | tf_op jit(solution)/shard_map/pallas_call | solution.py:443
  84.3 115.3 %shard_map.335 = (bf16[32,32,8192]{2,1,0:T(8,128)(2,1)}, bf16[32,128,1024]{2,1,0:T(8,128)(2,1)}) custom-call(bf16[32,8192]{1,0:T(8,128)(2,1)} %slice_bitcast_fusion.refs_0_, bf16[128,1024]{1,0:T(8,128)(2,1)} %convert_bitcast_fusion.refs_1_), custom_call_target="tpu_custom_call" | custom-call | tf_op jit(solution)/shard_map/pallas_call | solution.py:265
  201.1 4.8 fusion.18
  206.7 3.5 fusion.115
  210.2 2.7 convolution_convert_fusion.6
  212.9 2.6 fusion.105
  215.9 6.4 %fusion.9 = f32[256,4096]{1,0:T(8,128)S(1)} fusion(bf16[1024,8192]{1,0:T(8,128)(2,1)} %bitcast.209, f32[4096]{0:T(1024)S(1)} %add.402, f32[256,1024]{1,0:T(8,128)S(1)} %get-tuple-element.126, f32[1024]{0:T(1024)S(1)} %bitcast.221, f32[1024]{0:T(1024)S(1)} %bitcast.217, f32[256]{0:T(256)S(1)} %add_rsqrt_fusion.1, f32[256]{0:T(256)S(1)} %broadcast_multiply_fusion.7), kind=kOutput, calls=%fused_computation.16 | convolution fusion | flops 2149842944 | bytes 13658112 | tf_op jit(solution)/shard_map/dot_general | solution.py:41
  222.3 2.9 fusion.104
  229.0 16.3 %convert_reduce_fusion = (f32[4096]{0:T(1024)}, bf16[256,4096]{1,0:T(8,128)(2,1)S(1)}) fusion(bf16[256,1024]{1,0:T(8,128)(2,1)S(1)} %get-tuple-element.118, bf16[4096,1024]{1,0:T(8,128)(2,1)S(1)} %bitcast.242, f32[256,4096]{1,0:T(8,128)} %copy-done.84), kind=kOutput, calls=%fused_computation.20 | convolution fusion | flops 2168451072 | bytes 15220736 | tf_op jit(solution)/shard_map/dot_general | solution.py:51
  245.3 6.5 %multiply_reduce_fusion.6 = (bf16[1024]{0:T(1024)(128)(2,1)}, f32[256]{0:T(256)S(1)}, f32[256]{0:T(256)S(1)}, bf16[1024]{0:T(1024)(128)(2,1)}, f32[256,1024]{1,0:T(8,128)S(1)}) fusion(f32[256,1024]{1,0:T(8,128)S(1)} %get-tuple-element.126, f32[256]{0:T(256)S(1)} %add_rsqrt_fusion.1, f32[256]{0:T(256)S(1)} %broadcast_multiply_fusion.7, ...), kind=kOutput, calls=%fused_computation.74 | convolution fusion | flops 2149840384 | bytes 12595200 | tf_op jit(solution)/shard_map/dot_general | solution.py:51
  251.9 2.2 convert_reduce_fusion.4
  254.0 3.3 fusion.34
  259.4 3.3 multiply_reduce_fusion
  267.4 6.4 %multiply_reduce_fusion.3 = (f32[256]{0:T(256)}, bf16[1024]{0:T(1024)(128)(2,1)}, f32[256]{0:T(256)S(1)}, bf16[1024]{0:T(1024)(128)(2,1)}, f32[256,1024]{1,0:T(8,128)}) fusion(f32[256,1024]{1,0:T(8,128)S(1)} %get-tuple-element.172, f32[1024]{0:T(1024)S(1)} %bitcast.214, f32[256]{0:T(256)S(1)} %add_rsqrt_fusion.2, f32[256]{0:T(256)S(1)} %broadcast_multiply_fusion.8, ...), kind=kOutput, calls=%fused_computation.69 | convolution fusion | flops 1617688064 | bytes 9973760 | tf_op jit(solution)/shard_map/dot_general | solution.py:51
  277.8 2.1 convert_reduce_fusion.2
  286.1 11.9 %shard_map.337 = bf16[32,64,128]{2,1,0:T(8,128)(2,1)S(1)} custom-call(bf16[64,128]{1,0:T(8,128)(2,1)S(1)} %bitcast.172), custom_call_target="tpu_custom_call" | custom-call | tf_op jit(solution)/shard_map/pallas_call | solution.py:443
  298.0 2.3 reshape_reshape.3
  302.8 18.1 %shard_map.338 = f32[32,32,32]{2,1,0:T(8,128)S(1)} custom-call(f32[32,32,32]{2,1,0:T(8,128)S(1)} %bitcast.165), custom_call_target="tpu_custom_call" | custom-call | tf_op jit(solution)/shard_map/pallas_call | solution.py:443
  324.7 2.2 concatenate.135
  327.0 29.8 %shard_map.339 = (f32[32,32,32]{2,1,0:T(8,128)S(1)}, f32[32,41,32]{2,1,0:T(8,128)S(1)}, f32[32,1,128]{2,1,0:T(1,128)S(1)}) custom-call(f32[32,32,32]{2,1,0:T(8,128)S(1)} %bitcast.164, f32[32,41,32]{2,1,0:T(8,128)S(1)} %bitcast.163, f32[1,128]{1,0:T(1,128)S(1)} %fusion.89.refs_2_), custom_call_target="tpu_custom_call" | custom-call | tf_op jit(solution)/shard_map/pallas_call | solution.py:443
  360.3 6.3 %convolution_convert_fusion.3 = bf16[1024,3072]{1,0:T(8,128)(2,1)} fusion(bf16[256,1024]{0,1:T(8,128)(2,1)} %bitcast.186, bf16[256,1024]{0,1:T(8,128)(2,1)} %bitcast.183, bf16[256,1024]{0,1:T(8,128)(2,1)S(1)} %bitcast.180, f32[256,1024]{1,0:T(8,128)} %copy-done, f32[1024]{0:T(1024)S(1)} %bitcast.224, f32[1024]{0:T(1024)S(1)} %bitcast.216, ...), kind=kOutput, calls=%fused_computation.10 | convolution fusion | flops 1619787776 | bytes 8923136 | tf_op jit(solution)/shard_map/dot_general | solution.py:45
  366.6 2.1 convolution_convert_fusion.4
  369.0 5.7 %convolution_convert_fusion = bf16[1024,4096]{1,0:T(8,128)(2,1)} fusion(bf16[256,4096]{1,0:T(8,128)(2,1)S(1)} %copy-done.12, f32[256,1024]{1,0:T(8,128)S(1)} %copy-done.2, f32[1024]{0:T(1024)S(1)} %bitcast.222, f32[1024]{0:T(1024)S(1)} %bitcast.220, f32[256]{0:T(256)S(1)} %copy-done.64, f32[256]{0:T(256)S(1)} %copy-done.58), kind=kOutput, calls=%fused_computation.1 | convolution fusion | flops 2152988672 | bytes 11544576 | tf_op jit(solution)/shard_map/dot_general | solution.py:45
  374.8 5.4 convolution_convert_fusion.1
  382.6 136.1 %shard_map.340 = (f32[128,1024]{1,0:T(8,128)}, f32[32,4096]{1,0:T(8,128)}, f32[32,1024]{1,0:T(8,128)}, f32[32,3072]{1,0:T(8,128)}) custom-call(bf16[32,128,1024]{2,1,0:T(8,128)(2,1)} %bitcast.176, bf16[32,32,4096]{2,1,0:T(8,128)(2,1)} %bitcast.174, bf16[32,32,1024]{2,1,0:T(8,128)(2,1)} %bitcast.177, bf16[32,32,3072]{2,1,0:T(8,128)(2,1)} %bitcast.175), custom_call_target="tpu_custom_call" | custom-call | tf_op jit(solution)/shard_map/pallas_call | solution.py:390
  520.5 2.4 multiply_reduce_fusion.2
  525.5 8.3 %shard_map.341 = f32[32,1,128]{2,1,0:T(1,128)S(1)} custom-call(f32[1,128]{1,0:T(1,128)S(1)} %broadcast_in_dim.34.refs_0_), custom_call_target="tpu_custom_call" | custom-call | tf_op jit(solution)/shard_map/pallas_call | solution.py:443
  539.2 2.8 multiply_subtract_fusion.1
  543.6 3.3 multiply_subtract_fusion
  (341 shorter events, 63.8 us)
Async XLA Ops:
  0.7 41.9 %copy-start.3 = (f32[1,32,14336]{2,1,0:T(8,128)S(1)}, f32[1,32,14336]{2,1,0:T(8,128)}, u32[]{:S(2)}) copy-start(f32[1,32,14336]{2,1,0:T(8,128)} %param.26) | copy-start | bytes 5505028
  2.2 197.4 %collective-permute-start = (f32[128,32]{0,1:T(8,128)}, f32[128,32]{0,1:T(8,128)}, u32[]{:S(2)}, u32[]{:S(2)}) collective-permute-start(f32[128,32]{0,1:T(8,128)} %get-tuple-element.141), channel_id=1, source_target_pairs={{0,1},{1,0},{2,3},{3,2},{4,5},{5,4},{6,7},{7,6},{8,9},{9,8},{10,11... | collective-permute-start | bytes 49160 | tf_op jit(solution)/shard_map/ppermute | solution.py:538
  6.5 59.7 %copy-start.8 = (bf16[4361,32]{1,0:T(8,128)(2,1)}, bf16[4361,32]{1,0:T(8,128)(2,1)S(1)}, u32[]{:S(2)}) copy-start(bf16[4361,32]{1,0:T(8,128)(2,1)S(1)} %copy.129) | copy-start | bytes 837316
  42.5 22.3 %copy-start.16 = (f32[1,128,1024]{2,1,0:T(8,128)S(1)}, f32[1,128,1024]{2,1,0:T(8,128)}, u32[]{:S(2)}) copy-start(f32[1,128,1024]{2,1,0:T(8,128)} %param.27) | copy-start | bytes 1572868
  42.7 22.1 %copy-start.50 = (f32[32,32]{1,0:T(8,128)S(1)}, f32[32,32]{1,0:T(8,128)}, u32[]{:S(2)}) copy-start(f32[32,32]{1,0:T(8,128)} %get-tuple-element.92) | copy-start | bytes 12292
  42.7 22.1 %copy-start.49 = (f32[32,32]{1,0:T(8,128)S(1)}, f32[32,32]{1,0:T(8,128)}, u32[]{:S(2)}) copy-start(f32[32,32]{1,0:T(8,128)} %get-tuple-element.91) | copy-start | bytes 12292
  42.7 23.3 %copy-start.81 = (f32[32]{0:T(128)S(1)}, f32[32]{0:T(128)}, u32[]{:S(2)}) copy-start(f32[32]{0:T(128)} %get-tuple-element.153) | copy-start | bytes 388
  43.5 22.7 %copy-start.80 = (f32[32]{0:T(128)S(1)}, f32[32]{0:T(128)}, u32[]{:S(2)}) copy-start(f32[32]{0:T(128)} %get-tuple-element.152) | copy-start | bytes 388
  43.5 34.8 %copy-start.70 = (f32[256]{0:T(256)S(1)}, f32[256]{0:T(256)}, u32[]{:S(2)}) copy-start(f32[256]{0:T(256)} %get-tuple-element.187) | copy-start | bytes 3076
  43.5 34.8 %copy-start.71 = (f32[256]{0:T(256)S(1)}, f32[256]{0:T(256)}, u32[]{:S(2)}) copy-start(f32[256]{0:T(256)} %get-tuple-element.188) | copy-start | bytes 3076
  43.5 34.8 %copy-start.77 = (f32[256]{0:T(256)S(1)}, f32[256]{0:T(256)}, u32[]{:S(2)}) copy-start(f32[256]{0:T(256)} %negate_power_fusion) | copy-start | bytes 3076
  44.8 36.4 %copy-start.79 = (s32[32,1]{0,1:T(1,128)S(1)}, s32[32,1]{0,1:T(1,128)}, u32[]{:S(2)}) copy-start(s32[32,1]{0,1:T(1,128)} %get-tuple-element.160) | copy-start | bytes 388
  44.8 37.8 %copy-start.48 = (f32[32,32]{1,0:T(8,128)S(1)}, f32[32,32]{1,0:T(8,128)}, u32[]{:S(2)}) copy-start(f32[32,32]{1,0:T(8,128)} %get-tuple-element.93) | copy-start | bytes 12292
  44.8 37.9 %copy-start.38 = (bf16[16,32,32]{2,0,1:T(8,128)(2,1)S(1)}, bf16[16,32,32]{2,0,1:T(8,128)(2,1)}, u32[]{:S(2)}) copy-start(bf16[16,32,32]{2,0,1:T(8,128)(2,1)} %get-tuple-element.136) | copy-start | bytes 98308
  44.8 38.1 %copy-start.47 = (f32[32,32]{1,0:T(8,128)S(1)}, f32[32,32]{1,0:T(8,128)}, u32[]{:S(2)}) copy-start(f32[32,32]{1,0:T(8,128)} %get-tuple-element.90) | copy-start | bytes 12292
  44.9 38.2 %copy-start.46 = (f32[32,32]{1,0:T(8,128)S(1)}, f32[32,32]{1,0:T(8,128)}, u32[]{:S(2)}) copy-start(f32[32,32]{1,0:T(8,128)} %get-tuple-element.89) | copy-start | bytes 12292
  44.9 38.4 %copy-start.37 = (bf16[16,32,32]{2,0,1:T(8,128)(2,1)S(1)}, bf16[16,32,32]{2,0,1:T(8,128)(2,1)}, u32[]{:S(2)}) copy-start(bf16[16,32,32]{2,0,1:T(8,128)(2,1)} %get-tuple-element.137) | copy-start | bytes 98308
  64.0 135.6 %copy-start.51 = (f32[128,32]{0,1:T(8,128)S(1)}, f32[128,32]{0,1:T(8,128)}, u32[]{:S(2)}) copy-start(f32[128,32]{0,1:T(8,128)} %get-tuple-element.140) | copy-start | bytes 49156
  200.8 76.9 %copy-start = (f32[256,1024]{1,0:T(8,128)}, f32[256,1024]{1,0:T(8,128)S(1)}, u32[]{:S(2)}) copy-start(f32[256,1024]{1,0:T(8,128)S(1)} %get-tuple-element.172) | copy-start | bytes 3145732
  200.8 66.3 %copy-start.55 = (f32[256]{0:T(256)}, f32[256]{0:T(256)S(1)}, u32[]{:S(2)}) copy-start(f32[256]{0:T(256)S(1)} %broadcast_multiply_fusion.8) | copy-start | bytes 3076
  201.1 66.0 %copy-start.59 = (f32[256]{0:T(256)}, f32[256]{0:T(256)S(1)}, u32[]{:S(2)}) copy-start(f32[256]{0:T(256)S(1)} %add_rsqrt_fusion.2) | copy-start | bytes 3076
  215.5 36.3 %copy-start.1 = (f32[256,1024]{1,0:T(8,128)}, f32[256,1024]{1,0:T(8,128)S(1)}, u32[]{:S(2)}) copy-start(f32[256,1024]{1,0:T(8,128)S(1)} %get-tuple-element.126) | copy-start | bytes 3145732
  215.5 36.3 %copy-start.57 = (f32[256]{0:T(256)}, f32[256]{0:T(256)S(1)}, u32[]{:S(2)}) copy-start(f32[256]{0:T(256)S(1)} %broadcast_multiply_fusion.7) | copy-start | bytes 3076
  215.8 36.0 %copy-start.63 = (f32[256]{0:T(256)}, f32[256]{0:T(256)S(1)}, u32[]{:S(2)}) copy-start(f32[256]{0:T(256)S(1)} %add_rsqrt_fusion.1) | copy-start | bytes 3076
  279.9 21.6 %copy-start.9 = (bf16[4361,32]{1,0:T(8,128)(2,1)S(1)}, bf16[4361,32]{1,0:T(8,128)(2,1)}, u32[]{:S(2)}) copy-start(bf16[4361,32]{1,0:T(8,128)(2,1)} %copy-done.8) | copy-start | bytes 837316
  302.8 21.9 %copy-start.82 = (f32[16]{0:T(128)S(1)}, f32[16]{0:T(128)}, u32[]{:S(2)}) copy-start(f32[16]{0:T(128)} %get-tuple-element.95) | copy-start | bytes 196
  302.8 22.0 %copy-start.32 = (f32[16,32,32]{2,0,1:T(8,128)S(1)}, f32[16,32,32]{2,0,1:T(8,128)}, u32[]{:S(2)}) copy-start(f32[16,32,32]{2,0,1:T(8,128)} %copy.153) | copy-start | bytes 196612
  323.5 36.7 %copy-start.56 = (f32[256]{0:T(256)S(1)}, f32[256]{0:T(256)}, u32[]{:S(2)}) copy-start(f32[256]{0:T(256)} %copy-done.55) | copy-start | bytes 3076
  382.6 153.9 %copy-start.76 = (f32[16]{0:T(128)S(1)}, f32[16]{0:T(128)}, u32[]{:S(2)}) copy-start(f32[16]{0:T(128)} %param.30) | copy-start | bytes 196
  382.6 155.2 %copy-start.52 = (f32[19,32]{1,0:T(8,128)S(1)}, f32[19,32]{1,0:T(8,128)}, u32[]{:S(2)}) copy-start(f32[19,32]{1,0:T(8,128)} %param.29) | copy-start | bytes 7300
  382.6 156.6 %copy-start.10 = (f32[4361,32]{0,1:T(8,128)S(1)}, f32[4361,32]{0,1:T(8,128)}, u32[]{:S(2)}) copy-start(f32[4361,32]{0,1:T(8,128)} %param.28) | copy-start | bytes 1674628
  520.5 21.6 %copy-start.39 = (f32[1,128,1024]{2,1,0:T(8,128)S(1)}, f32[1,128,1024]{2,1,0:T(8,128)}, u32[]{:S(2)}) copy-start(f32[1,128,1024]{2,1,0:T(8,128)} %param.34) | copy-start | bytes 1572868
  (59 other events, 392.9 us)
